TPU v7x, 256 devices: a whole 4x4x8 slice. The times are simulated.
256 devices in a mesh: sta: 4 (over x), clu: 64 (over z, y, core).
Axes of the slice: x: 4, y: 4, z: 8, core: 2. Of those that a mesh axis runs over, the one named last changes fastest.
Arguments:
- spectra: bfloat16 [2048, 256, 128], P('clu', 'sta'), may hold values from -6 to 6
- partials: bfloat16 [2048, 4, 256], P('clu', None, 'sta')
- pair_list: int32 [2048, 50], P('clu'), may hold values from -1 to 103, as said below
- station_mask: int32 [2048, 50, 256], P('clu', None, 'sta'), may hold values 0 or 1
- exports: int32 [384, 12], P('clu'), may hold values from 0 to 31
Outputs:
- normal_blocks: float32 [16, 51, 2048], P('sta', None, 'clu')
- right_sides: float32 [4, 2048], P('sta', 'clu')
Inputs may be any that keep to these rules, and one draw needn't show every extreme that they name: `pair_list`: each event's valid entries come first and the rest are -1; every event has 25 to 50 valid entries and the first event of every cluster has all 50. A valid entry below 32 names an event of the same cluster; entry 32 + h * 12 + c names the c-th event sent to this cluster by the cluster at cycle offset -o(h) from it, o(h) as for exports.
All inputs are finite; a program needn't handle non-finite values. No bound on the sum of `station_mask` on one device may be relied on, other than what follows from the above.
Results may differ from a plain program's by a relative error of at most 0.0047.
Values may be sent and summed in bfloat16 or wider, within the bound.
A program may use at most 64 MiB of HBM per device.

v0:
```python
import math

import jax
import jax.numpy as jnp
from jax import lax
from jax.sharding import PartitionSpec as P


def shifted(block, axis, distance):
    devices = range(lax.axis_size(axis))
    route = [((i - distance) % len(devices), i) for i in devices]
    return lax.ppermute(block, axis, route)


def lag_tables(freq_count):
    freq_values = jnp.arange(freq_count, dtype=jnp.float32) * (math.pi / freq_count)
    lag_values = jnp.arange(2 * freq_count - 1, dtype=jnp.float32) - (freq_count - 1)
    phase_grid = freq_values[:, None] * lag_values[None, :]
    cosine_grid = jnp.cos(phase_grid)
    sine_grid = jnp.sin(phase_grid)
    real_rows = jnp.concatenate([cosine_grid, -freq_values[:, None] * sine_grid], axis=1)
    imag_rows = jnp.concatenate([-sine_grid, -freq_values[:, None] * cosine_grid], axis=1)
    lag_table = jnp.concatenate([real_rows, imag_rows], axis=0).astype(jnp.bfloat16)
    return (lag_table, lag_values)


def pair_weights(spec_one, spec_two, energy_one, energy_two, lag_table, lag_values, freq_count):
    first_vals = spec_one.astype(jnp.float32)
    second_vals = spec_two.astype(jnp.float32)
    real_a = first_vals[..., :freq_count]
    imag_a = first_vals[..., freq_count:]
    real_b = second_vals[..., :freq_count]
    imag_b = second_vals[..., freq_count:]
    cross_spec = jnp.concatenate(
        [real_a * real_b + imag_a * imag_b, imag_a * real_b - real_a * imag_b], axis=-1
    ).astype(jnp.bfloat16)
    lead_shape = cross_spec.shape[:-1]
    lagged = jnp.dot(
        cross_spec.reshape(-1, 2 * freq_count), lag_table, preferred_element_type=jnp.float32
    )
    lag_count = lag_values.shape[0]
    inverse = lax.rsqrt((energy_one * energy_two).reshape(-1) + 1e-06)
    correlation = lagged[:, :lag_count] * inverse[:, None]
    slope_fn = lagged[:, lag_count:] * inverse[:, None]
    power_sum = jnp.sum(correlation * correlation, axis=1)
    rough_sum = jnp.sum(slope_fn * slope_fn, axis=1)
    delay_lag = jnp.sum(correlation * correlation * lag_values[None, :], axis=1) / (
        power_sum + 1e-06
    )
    weight = power_sum / (power_sum + 0.125 * rough_sum + 1e-06)
    return (weight.reshape(lead_shape), delay_lag.reshape(lead_shape))


def on_device(spectra, partials, pair_list, station_mask, exports):
    highest = lax.Precision.HIGHEST
    event_count, station_count, two_freq = spectra.shape
    freq_count = two_freq // 2
    sta_groups = lax.axis_size("sta")
    groups_out = exports.shape[0]
    half_span = groups_out // 2
    capacity = exports.shape[1]
    neighbours = pair_list.shape[1]
    all_stations = station_count * sta_groups
    offsets = [h - half_span + (1 if h >= half_span else 0) for h in range(groups_out)]
    lag_table, lag_values = lag_tables(freq_count)
    energy = jnp.sum(jnp.square(spectra.astype(jnp.float32)), axis=-1)
    spec_len = station_count * two_freq
    outgoing = jnp.concatenate(
        [
            spectra[exports].reshape(groups_out, capacity, spec_len),
            partials[exports].reshape(groups_out, capacity, 4 * station_count),
        ],
        axis=2,
    )
    received = [None] * groups_out
    for h in range(groups_out):
        received[h] = shifted(outgoing[h], "clu", offsets[h])
    got_rows = jnp.stack(received, axis=0)
    imported = groups_out * capacity
    got_spec = got_rows[..., :spec_len].reshape(imported, station_count, two_freq)
    got_geo = got_rows[..., spec_len:].reshape(imported, 4, station_count)
    got_energy = jnp.sum(jnp.square(got_spec.astype(jnp.float32)), axis=-1)
    cand_spec = jnp.concatenate([spectra, got_spec], axis=0)
    cand_geo = jnp.concatenate([partials, got_geo], axis=0)
    cand_energy = jnp.concatenate([energy, got_energy], axis=0)
    cand_total = event_count + imported
    cand_ids = jnp.arange(cand_total, dtype=jnp.int32)
    live_pairs = (pair_list >= 0).astype(jnp.float32)[..., None] * station_mask.astype(jnp.float32)
    clipped = jnp.maximum(pair_list, 0)
    block_size = max(event_count // 16, 1)
    rounds = event_count // block_size

    def one_round(accumulated, inputs):
        acc_diag, acc_right = accumulated
        spec_a, geo_a, energy_a, partner_b, live_b = inputs
        weight, delay_lag = pair_weights(
            spec_a[:, None],
            cand_spec[partner_b],
            energy_a[:, None],
            cand_energy[partner_b],
            lag_table,
            lag_values,
            freq_count,
        )
        scaled = weight * live_b / all_stations
        geo_one = geo_a.astype(jnp.float32)
        geo_two = cand_geo[partner_b].astype(jnp.float32)
        diag_one = jnp.einsum(
            "rks,ris,rjs->ijr", scaled, geo_one, geo_one, precision=highest
        ).reshape(16, -1)
        off_diag = -jnp.einsum(
            "rks,ris,rkjs->ijkr", scaled, geo_one, geo_two, precision=highest
        ).reshape(16, neighbours, -1)
        right_one = jnp.einsum("rks,ris->ir", scaled * delay_lag, geo_one, precision=highest)
        diag_two = jnp.einsum(
            "rks,rkis,rkjs->rkij", scaled, geo_two, geo_two, precision=highest
        ).reshape(-1, 16)
        right_two = -jnp.einsum(
            "rks,rkis->rki", scaled * delay_lag, geo_two, precision=highest
        ).reshape(-1, 4)
        onehot = (partner_b.reshape(-1)[:, None] == cand_ids[None, :]).astype(jnp.float32)
        acc_diag = acc_diag + jnp.dot(diag_two.T, onehot, precision=highest)
        acc_right = acc_right + jnp.dot(right_two.T, onehot, precision=highest)
        return ((acc_diag, acc_right), (diag_one, off_diag, right_one))

    round_inputs = (
        spectra.reshape(rounds, block_size, station_count, two_freq),
        partials.reshape(rounds, block_size, 4, station_count),
        energy.reshape(rounds, block_size, station_count),
        clipped.reshape(rounds, block_size, neighbours),
        live_pairs.reshape(rounds, block_size, neighbours, station_count),
    )
    start_acc = (jnp.zeros((16, cand_total), jnp.float32), jnp.zeros((4, cand_total), jnp.float32))
    (acc_diag, acc_right), (diag_rows, off_rows, right_rows) = lax.scan(
        one_round, start_acc, round_inputs
    )
    diagonal = diag_rows.transpose(1, 0, 2).reshape(16, event_count) + acc_diag[:, :event_count]
    off_blocks = off_rows.transpose(1, 2, 0, 3).reshape(16, neighbours, event_count)
    right_hand = right_rows.transpose(1, 0, 2).reshape(4, event_count) + acc_right[:, :event_count]
    import_diag = acc_diag[:, event_count:].reshape(16, groups_out, capacity)
    import_right = acc_right[:, event_count:].reshape(4, groups_out, capacity)
    owner_hot = (
        exports.reshape(-1)[:, None] == jnp.arange(event_count, dtype=jnp.int32)[None, :]
    ).astype(jnp.float32)

    def spread(values):
        return jnp.dot(values.reshape(values.shape[0], -1), owner_hot, precision=highest)

    import_terms = jnp.concatenate([import_diag, import_right], axis=0)
    back_list = [shifted(import_terms[:, h], "clu", -offsets[h]) for h in range(groups_out)]
    back_terms = jnp.stack(back_list, axis=1)
    diagonal = diagonal + spread(back_terms[:16])
    right_hand = right_hand + spread(back_terms[16:])
    normal_part = jnp.concatenate([diagonal[:, None, :], off_blocks], axis=1)
    total_normal, total_right = lax.psum((normal_part, right_hand), "sta")
    sta_place = lax.axis_index("sta")
    normal_share = lax.dynamic_slice_in_dim(
        total_normal, sta_place * (16 // sta_groups), 16 // sta_groups, 0
    )
    right_share = lax.dynamic_slice_in_dim(
        total_right, sta_place * (4 // sta_groups), 4 // sta_groups, 0
    )
    return (normal_share, right_share)


def solution(mesh):
    return jax.shard_map(
        on_device,
        mesh=mesh,
        in_specs=(
            P("clu", "sta", None),
            P("clu", None, "sta"),
            P("clu", None),
            P("clu", None, "sta"),
            P("clu", None),
        ),
        out_specs=(P("sta", None, "clu"), P("sta", "clu")),
        check_vma=False,
    )
```

profile of v0, /device:TPU:1, one launch (start us, length us, event | category | flops | bytes accessed | tf_op | source)
XLA Modules:
  0.0 459.6 jit_solution(10548839486217955144)
XLA Ops:
  8.0 1.8 gather_fusion.3
  13.2 9.4 %collective-permute-start = (bf16[12,8448]{1,0:T(8,128)(2,1)}, bf16[12,8448]{1,0:T(8,128)(2,1)S(1)}, u32[]{:S(2)}, u32[]{:S(2)}) collective-permute-start(bf16[12,8448]{1,0:T(8,128)(2,1)} %get-tuple-element.287), channel_id=1, source_target_pairs={{3,0},{4,1},{5,2},{6,3},{7,4},{8,5},{9,6},{10,7},{11,8},{12,9},{13... | collective-permute-start | bytes 608264 | tf_op jit(solution)/shard_map/ppermute | solution.py:12
  25.8 1.4 multiply_reduce_fusion.3
  30.4 4.4 collective-permute-done.1
  34.9 2.1 collective-permute-done.2
  37.0 5.3 %collective-permute-done.4 = bf16[12,8448]{1,0:T(8,128)(2,1)S(1)} collective-permute-done((bf16[12,8448]{1,0:T(8,128)(2,1)S(1)}, bf16[12,8448]{1,0:T(8,128)(2,1)S(1)}, u32[]{:S(2)}, u32[]{:S(2)}) %collective-permute-start.4) | collective-permute-done | bytes 202784 | tf_op jit(solution)/shard_map/ppermute | solution.py:12
  42.4 1.4 collective-permute-done.5
  46.7 1.2 pad_maximum_fusion
  48.9 332.7 %while.19 = (s32[]{:T(128)}, f32[16,104]{1,0:T(8,128)}, f32[4,104]{1,0:T(4,128)}, f32[16,16,2]{1,2,0:T(2,128)}, f32[16,16,50,2]{2,1,3,0:T(8,128)}, /*index=5*/f3...) while((s32[]{:T(128)}, f32[16,104]{1,0:T(8,128)}, ...), condition=%wide.region_8.9_spmd.clone, body=%wide.region_2.8_spmd.clone.sunk | while | flops 435276384 | bytes 30170480 | solution.py:134
  51.7 1.2 add_convert_fusion.2
  53.0 3.9 fusion.76
  58.1 4.2 multiply_reduce_fusion.6
  72.6 1.2 add_convert_fusion.2
  73.8 3.9 fusion.76
  78.9 4.2 multiply_reduce_fusion.6
  93.3 1.2 add_convert_fusion.2
  94.5 3.9 fusion.76
  99.6 4.2 multiply_reduce_fusion.6
  114.1 1.2 add_convert_fusion.2
  115.3 3.9 fusion.76
  120.5 4.2 multiply_reduce_fusion.6
  134.9 1.2 add_convert_fusion.2
  136.1 3.9 fusion.76
  141.3 4.2 multiply_reduce_fusion.6
  155.6 1.2 add_convert_fusion.2
  156.9 3.9 fusion.76
  162.0 4.2 multiply_reduce_fusion.6
  176.5 1.2 add_convert_fusion.2
  177.7 3.9 fusion.76
  182.8 4.2 multiply_reduce_fusion.6
  197.3 1.2 add_convert_fusion.2
  198.5 3.9 fusion.76
  203.6 4.2 multiply_reduce_fusion.6
  218.1 1.2 add_convert_fusion.2
  219.3 3.9 fusion.76
  224.5 4.2 multiply_reduce_fusion.6
  238.9 1.2 add_convert_fusion.2
  240.2 3.9 fusion.76
  245.3 4.2 multiply_reduce_fusion.6
  259.7 1.2 add_convert_fusion.2
  260.9 3.9 fusion.76
  266.0 4.2 multiply_reduce_fusion.6
  280.5 1.2 add_convert_fusion.2
  281.7 3.9 fusion.76
  286.8 4.2 multiply_reduce_fusion.6
  301.2 1.2 add_convert_fusion.2
  302.5 3.9 fusion.76
  307.6 4.2 multiply_reduce_fusion.6
  322.0 1.2 add_convert_fusion.2
  323.2 3.9 fusion.76
  328.3 4.2 multiply_reduce_fusion.6
  342.8 1.2 add_convert_fusion.2
  344.0 3.9 fusion.76
  349.1 4.2 multiply_reduce_fusion.6
  363.6 1.2 add_convert_fusion.2
  364.8 3.9 fusion.76
  370.0 4.2 multiply_reduce_fusion.6
  383.7 2.4 collective-permute-start.8
  386.7 4.7 %collective-permute-start.10 = (f32[20,12]{0,1:T(8,128)S(1)}, f32[20,12]{0,1:T(8,128)S(1)}, u32[]{:S(2)}, u32[]{:S(2)}) collective-permute-start(f32[20,12]{0,1:T(8,128)S(1)} %bitcast.197), channel_id=1, source_target_pairs={{2,0},{3,1},{4,2},{5,3},{6,4},{7,5},{8,6},{9,7},{10,8},{11,9},{12,... | collective-permute-start | bytes 2888 | tf_op jit(solution)/shard_map/ppermute | solution.py:12
  394.2 1.6 collective-permute-start.11
  395.9 3.0 collective-permute-done.11
  400.0 8.5 %psum.15 = f32[4,32]{1,0:T(4,128)S(1)} all-reduce(f32[4,32]{1,0:T(4,128)S(1)} %convolution_add_fusion.3), channel_id=1, replica_groups=mesh['sta'=4,'clu'=64] {'sta'}, use_global_device_ids=true, to_apply=%region_10.11 | all-reduce | flops 128 | bytes 1024 | tf_op jit(solution)/shard_map/psum | solution.py:155
  411.0 40.3 %all-reduce.2.cloned.1.call-done = f32[16,51,32]{1,2,0:T(8,128)} async-done(((f32[16,51,32]{1,2,0:T(8,128)}), f32[16,51,32]{1,2,0:T(8,128)}) %all-reduce.2.cloned.1.call-update) | async-done | bytes 104464 | tf_op jit(solution)/shard_map/psum | solution.py:155
  451.3 1.5 constant_dynamic-slice_fusion.4
  (1182 shorter events, 205.2 us)
Async XLA Ops:
  7.2 444.1 %all-reduce.2.cloned.1.call-start = ((), (), s32[]{:S(2)}) async-start(), calls=%async_computation | async-start | bytes 524288 | tf_op jit(solution)/shard_map/psum | solution.py:155
  12.2 15.0 %copy-start.8 = (s32[6,12]{1,0:T(8,128)S(1)}, s32[6,12]{1,0:T(8,128)}, u32[]{:S(2)}) copy-start(s32[6,12]{1,0:T(8,128)} %param.11) | copy-start | bytes 868
  12.2 15.7 %copy-start.4 = (s32[32,50]{1,0:T(8,128)S(1)}, s32[32,50]{1,0:T(8,128)}, u32[]{:S(2)}) copy-start(s32[32,50]{1,0:T(8,128)} %param.9) | copy-start | bytes 19204
  12.2 15.7 %copy-start.2 = (s32[32,50,64]{2,0,1:T(8,128)S(1)}, s32[32,50,64]{2,0,1:T(8,128)}, u32[]{:S(2)}) copy-start(s32[32,50,64]{2,0,1:T(8,128)} %param.10) | copy-start | bytes 1228804
  13.2 16.9 %collective-permute-start = (bf16[12,8448]{1,0:T(8,128)(2,1)}, bf16[12,8448]{1,0:T(8,128)(2,1)S(1)}, u32[]{:S(2)}, u32[]{:S(2)}) collective-permute-start(bf16[12,8448]{1,0:T(8,128)(2,1)} %get-tuple-element.287), channel_id=1, source_target_pairs={{3,0},{4,1},{5,2},{6,3},{7,4},{8,5},{9,6},{10,7},{11,8},{12,9},{13... | collective-permute-start | bytes 608264 | tf_op jit(solution)/shard_map/ppermute | solution.py:12
  22.6 12.3 %collective-permute-start.1 = (bf16[12,8448]{1,0:T(8,128)(2,1)}, bf16[12,8448]{1,0:T(8,128)(2,1)S(1)}, u32[]{:S(2)}, u32[]{:S(2)}) collective-permute-start(bf16[12,8448]{1,0:T(8,128)(2,1)} %get-tuple-element.286), channel_id=1, source_target_pairs={{2,0},{3,1},{4,2},{5,3},{6,4},{7,5},{8,6},{9,7},{10,8},{11,9},{12,... | collective-permute-start | bytes 608264 | tf_op jit(solution)/shard_map/ppermute | solution.py:12
  23.0 13.9 %collective-permute-start.2 = (bf16[12,8448]{1,0:T(8,128)(2,1)}, bf16[12,8448]{1,0:T(8,128)(2,1)S(1)}, u32[]{:S(2)}, u32[]{:S(2)}) collective-permute-start(bf16[12,8448]{1,0:T(8,128)(2,1)} %get-tuple-element.285), channel_id=1, source_target_pairs={{1,0},{2,1},{3,2},{4,3},{5,4},{6,5},{7,6},{8,7},{9,8},{10,9},{11,1... | collective-permute-start | bytes 608264 | tf_op jit(solution)/shard_map/ppermute | solution.py:12
  23.6 13.3 %collective-permute-start.3 = (bf16[12,8448]{1,0:T(8,128)(2,1)S(1)}, bf16[12,8448]{1,0:T(8,128)(2,1)S(1)}, u32[]{:S(2)}, u32[]{:S(2)}) collective-permute-start(bf16[12,8448]{1,0:T(8,128)(2,1)S(1)} %get-tuple-element.284), channel_id=1, source_target_pairs={{63,0},{0,1},{1,2},{2,3},{3,4},{4,5},{5,6},{6,7},{7,8},{8,9},{9,10... | collective-permute-start | bytes 608264 | tf_op jit(solution)/shard_map/ppermute | solution.py:12
  24.8 17.6 %collective-permute-start.4 = (bf16[12,8448]{1,0:T(8,128)(2,1)S(1)}, bf16[12,8448]{1,0:T(8,128)(2,1)S(1)}, u32[]{:S(2)}, u32[]{:S(2)}) collective-permute-start(bf16[12,8448]{1,0:T(8,128)(2,1)S(1)} %get-tuple-element.283), channel_id=1, source_target_pairs={{62,0},{63,1},{0,2},{1,3},{2,4},{3,5},{4,6},{5,7},{6,8},{7,9},{8,1... | collective-permute-start | bytes 608264 | tf_op jit(solution)/shard_map/ppermute | solution.py:12
  30.1 13.7 %collective-permute-start.5 = (bf16[12,8448]{1,0:T(8,128)(2,1)S(1)}, bf16[12,8448]{1,0:T(8,128)(2,1)S(1)}, u32[]{:S(2)}, u32[]{:S(2)}) collective-permute-start(bf16[12,8448]{1,0:T(8,128)(2,1)S(1)} %get-tuple-element.282), channel_id=1, source_target_pairs={{61,0},{62,1},{63,2},{0,3},{1,4},{2,5},{3,6},{4,7},{5,8},{6,9},{7,... | collective-permute-start | bytes 608264 | tf_op jit(solution)/shard_map/ppermute | solution.py:12
  62.3 4.7 %copy-start.9 = (f32[16,104]{1,0:T(8,128)S(1)}, f32[16,104]{1,0:T(8,128)}, u32[]{:S(2)}) copy-start(f32[16,104]{1,0:T(8,128)} %get-tuple-element.434) | copy-start | bytes 19972 | tf_op jit(solution)/shard_map/while
  62.8 4.9 %copy-start.11 = (f32[4,104]{1,0:T(4,128)S(1)}, f32[4,104]{1,0:T(4,128)}, u32[]{:S(2)}) copy-start(f32[4,104]{1,0:T(4,128)} %get-tuple-element.435) | copy-start | bytes 4996 | tf_op jit(solution)/shard_map/while
  63.7 6.1 %copy-start.6 = (s32[16,2,50]{2,1,0:T(2,128)S(1)}, s32[16,2,50]{2,1,0:T(2,128)}, u32[]{:S(2)}) copy-start(s32[16,2,50]{2,1,0:T(2,128)} %copy-done.5) | copy-start | bytes 19204 | tf_op jit(solution)/shard_map/while
  83.1 4.7 %copy-start.9 = (f32[16,104]{1,0:T(8,128)S(1)}, f32[16,104]{1,0:T(8,128)}, u32[]{:S(2)}) copy-start(f32[16,104]{1,0:T(8,128)} %get-tuple-element.434) | copy-start | bytes 19972 | tf_op jit(solution)/shard_map/while
  83.6 4.9 %copy-start.11 = (f32[4,104]{1,0:T(4,128)S(1)}, f32[4,104]{1,0:T(4,128)}, u32[]{:S(2)}) copy-start(f32[4,104]{1,0:T(4,128)} %get-tuple-element.435) | copy-start | bytes 4996 | tf_op jit(solution)/shard_map/while
  84.5 6.0 %copy-start.6 = (s32[16,2,50]{2,1,0:T(2,128)S(1)}, s32[16,2,50]{2,1,0:T(2,128)}, u32[]{:S(2)}) copy-start(s32[16,2,50]{2,1,0:T(2,128)} %copy-done.5) | copy-start | bytes 19204 | tf_op jit(solution)/shard_map/while
  103.9 4.7 %copy-start.9 = (f32[16,104]{1,0:T(8,128)S(1)}, f32[16,104]{1,0:T(8,128)}, u32[]{:S(2)}) copy-start(f32[16,104]{1,0:T(8,128)} %get-tuple-element.434) | copy-start | bytes 19972 | tf_op jit(solution)/shard_map/while
  104.3 4.9 %copy-start.11 = (f32[4,104]{1,0:T(4,128)S(1)}, f32[4,104]{1,0:T(4,128)}, u32[]{:S(2)}) copy-start(f32[4,104]{1,0:T(4,128)} %get-tuple-element.435) | copy-start | bytes 4996 | tf_op jit(solution)/shard_map/while
  105.2 6.1 %copy-start.6 = (s32[16,2,50]{2,1,0:T(2,128)S(1)}, s32[16,2,50]{2,1,0:T(2,128)}, u32[]{:S(2)}) copy-start(s32[16,2,50]{2,1,0:T(2,128)} %copy-done.5) | copy-start | bytes 19204 | tf_op jit(solution)/shard_map/while
  124.7 4.7 %copy-start.9 = (f32[16,104]{1,0:T(8,128)S(1)}, f32[16,104]{1,0:T(8,128)}, u32[]{:S(2)}) copy-start(f32[16,104]{1,0:T(8,128)} %get-tuple-element.434) | copy-start | bytes 19972 | tf_op jit(solution)/shard_map/while
  125.1 4.9 %copy-start.11 = (f32[4,104]{1,0:T(4,128)S(1)}, f32[4,104]{1,0:T(4,128)}, u32[]{:S(2)}) copy-start(f32[4,104]{1,0:T(4,128)} %get-tuple-element.435) | copy-start | bytes 4996 | tf_op jit(solution)/shard_map/while
  126.0 6.1 %copy-start.6 = (s32[16,2,50]{2,1,0:T(2,128)S(1)}, s32[16,2,50]{2,1,0:T(2,128)}, u32[]{:S(2)}) copy-start(s32[16,2,50]{2,1,0:T(2,128)} %copy-done.5) | copy-start | bytes 19204 | tf_op jit(solution)/shard_map/while
  145.5 4.7 %copy-start.9 = (f32[16,104]{1,0:T(8,128)S(1)}, f32[16,104]{1,0:T(8,128)}, u32[]{:S(2)}) copy-start(f32[16,104]{1,0:T(8,128)} %get-tuple-element.434) | copy-start | bytes 19972 | tf_op jit(solution)/shard_map/while
  146.0 4.9 %copy-start.11 = (f32[4,104]{1,0:T(4,128)S(1)}, f32[4,104]{1,0:T(4,128)}, u32[]{:S(2)}) copy-start(f32[4,104]{1,0:T(4,128)} %get-tuple-element.435) | copy-start | bytes 4996 | tf_op jit(solution)/shard_map/while
  146.9 6.0 %copy-start.6 = (s32[16,2,50]{2,1,0:T(2,128)S(1)}, s32[16,2,50]{2,1,0:T(2,128)}, u32[]{:S(2)}) copy-start(s32[16,2,50]{2,1,0:T(2,128)} %copy-done.5) | copy-start | bytes 19204 | tf_op jit(solution)/shard_map/while
  166.2 4.7 %copy-start.9 = (f32[16,104]{1,0:T(8,128)S(1)}, f32[16,104]{1,0:T(8,128)}, u32[]{:S(2)}) copy-start(f32[16,104]{1,0:T(8,128)} %get-tuple-element.434) | copy-start | bytes 19972 | tf_op jit(solution)/shard_map/while
  166.7 4.9 %copy-start.11 = (f32[4,104]{1,0:T(4,128)S(1)}, f32[4,104]{1,0:T(4,128)}, u32[]{:S(2)}) copy-start(f32[4,104]{1,0:T(4,128)} %get-tuple-element.435) | copy-start | bytes 4996 | tf_op jit(solution)/shard_map/while
  167.6 6.1 %copy-start.6 = (s32[16,2,50]{2,1,0:T(2,128)S(1)}, s32[16,2,50]{2,1,0:T(2,128)}, u32[]{:S(2)}) copy-start(s32[16,2,50]{2,1,0:T(2,128)} %copy-done.5) | copy-start | bytes 19204 | tf_op jit(solution)/shard_map/while
  187.0 4.7 %copy-start.9 = (f32[16,104]{1,0:T(8,128)S(1)}, f32[16,104]{1,0:T(8,128)}, u32[]{:S(2)}) copy-start(f32[16,104]{1,0:T(8,128)} %get-tuple-element.434) | copy-start | bytes 19972 | tf_op jit(solution)/shard_map/while
  187.5 4.9 %copy-start.11 = (f32[4,104]{1,0:T(4,128)S(1)}, f32[4,104]{1,0:T(4,128)}, u32[]{:S(2)}) copy-start(f32[4,104]{1,0:T(4,128)} %get-tuple-element.435) | copy-start | bytes 4996 | tf_op jit(solution)/shard_map/while
  188.4 6.1 %copy-start.6 = (s32[16,2,50]{2,1,0:T(2,128)S(1)}, s32[16,2,50]{2,1,0:T(2,128)}, u32[]{:S(2)}) copy-start(s32[16,2,50]{2,1,0:T(2,128)} %copy-done.5) | copy-start | bytes 19204 | tf_op jit(solution)/shard_map/while
  207.9 4.7 %copy-start.9 = (f32[16,104]{1,0:T(8,128)S(1)}, f32[16,104]{1,0:T(8,128)}, u32[]{:S(2)}) copy-start(f32[16,104]{1,0:T(8,128)} %get-tuple-element.434) | copy-start | bytes 19972 | tf_op jit(solution)/shard_map/while
  208.3 4.9 %copy-start.11 = (f32[4,104]{1,0:T(4,128)S(1)}, f32[4,104]{1,0:T(4,128)}, u32[]{:S(2)}) copy-start(f32[4,104]{1,0:T(4,128)} %get-tuple-element.435) | copy-start | bytes 4996 | tf_op jit(solution)/shard_map/while
  209.2 6.1 %copy-start.6 = (s32[16,2,50]{2,1,0:T(2,128)S(1)}, s32[16,2,50]{2,1,0:T(2,128)}, u32[]{:S(2)}) copy-start(s32[16,2,50]{2,1,0:T(2,128)} %copy-done.5) | copy-start | bytes 19204 | tf_op jit(solution)/shard_map/while
  228.7 4.7 %copy-start.9 = (f32[16,104]{1,0:T(8,128)S(1)}, f32[16,104]{1,0:T(8,128)}, u32[]{:S(2)}) copy-start(f32[16,104]{1,0:T(8,128)} %get-tuple-element.434) | copy-start | bytes 19972 | tf_op jit(solution)/shard_map/while
  229.1 4.9 %copy-start.11 = (f32[4,104]{1,0:T(4,128)S(1)}, f32[4,104]{1,0:T(4,128)}, u32[]{:S(2)}) copy-start(f32[4,104]{1,0:T(4,128)} %get-tuple-element.435) | copy-start | bytes 4996 | tf_op jit(solution)/shard_map/while
  230.1 6.1 %copy-start.6 = (s32[16,2,50]{2,1,0:T(2,128)S(1)}, s32[16,2,50]{2,1,0:T(2,128)}, u32[]{:S(2)}) copy-start(s32[16,2,50]{2,1,0:T(2,128)} %copy-done.5) | copy-start | bytes 19204 | tf_op jit(solution)/shard_map/while
  249.5 4.7 %copy-start.9 = (f32[16,104]{1,0:T(8,128)S(1)}, f32[16,104]{1,0:T(8,128)}, u32[]{:S(2)}) copy-start(f32[16,104]{1,0:T(8,128)} %get-tuple-element.434) | copy-start | bytes 19972 | tf_op jit(solution)/shard_map/while
  250.0 4.9 %copy-start.11 = (f32[4,104]{1,0:T(4,128)S(1)}, f32[4,104]{1,0:T(4,128)}, u32[]{:S(2)}) copy-start(f32[4,104]{1,0:T(4,128)} %get-tuple-element.435) | copy-start | bytes 4996 | tf_op jit(solution)/shard_map/while
  250.9 6.0 %copy-start.6 = (s32[16,2,50]{2,1,0:T(2,128)S(1)}, s32[16,2,50]{2,1,0:T(2,128)}, u32[]{:S(2)}) copy-start(s32[16,2,50]{2,1,0:T(2,128)} %copy-done.5) | copy-start | bytes 19204 | tf_op jit(solution)/shard_map/while
  270.3 4.7 %copy-start.9 = (f32[16,104]{1,0:T(8,128)S(1)}, f32[16,104]{1,0:T(8,128)}, u32[]{:S(2)}) copy-start(f32[16,104]{1,0:T(8,128)} %get-tuple-element.434) | copy-start | bytes 19972 | tf_op jit(solution)/shard_map/while
  270.7 4.9 %copy-start.11 = (f32[4,104]{1,0:T(4,128)S(1)}, f32[4,104]{1,0:T(4,128)}, u32[]{:S(2)}) copy-start(f32[4,104]{1,0:T(4,128)} %get-tuple-element.435) | copy-start | bytes 4996 | tf_op jit(solution)/shard_map/while
  271.6 6.1 %copy-start.6 = (s32[16,2,50]{2,1,0:T(2,128)S(1)}, s32[16,2,50]{2,1,0:T(2,128)}, u32[]{:S(2)}) copy-start(s32[16,2,50]{2,1,0:T(2,128)} %copy-done.5) | copy-start | bytes 19204 | tf_op jit(solution)/shard_map/while
  291.1 4.7 %copy-start.9 = (f32[16,104]{1,0:T(8,128)S(1)}, f32[16,104]{1,0:T(8,128)}, u32[]{:S(2)}) copy-start(f32[16,104]{1,0:T(8,128)} %get-tuple-element.434) | copy-start | bytes 19972 | tf_op jit(solution)/shard_map/while
  291.5 4.9 %copy-start.11 = (f32[4,104]{1,0:T(4,128)S(1)}, f32[4,104]{1,0:T(4,128)}, u32[]{:S(2)}) copy-start(f32[4,104]{1,0:T(4,128)} %get-tuple-element.435) | copy-start | bytes 4996 | tf_op jit(solution)/shard_map/while
  292.4 6.0 %copy-start.6 = (s32[16,2,50]{2,1,0:T(2,128)S(1)}, s32[16,2,50]{2,1,0:T(2,128)}, u32[]{:S(2)}) copy-start(s32[16,2,50]{2,1,0:T(2,128)} %copy-done.5) | copy-start | bytes 19204 | tf_op jit(solution)/shard_map/while
  311.8 4.7 %copy-start.9 = (f32[16,104]{1,0:T(8,128)S(1)}, f32[16,104]{1,0:T(8,128)}, u32[]{:S(2)}) copy-start(f32[16,104]{1,0:T(8,128)} %get-tuple-element.434) | copy-start | bytes 19972 | tf_op jit(solution)/shard_map/while
  312.3 4.9 %copy-start.11 = (f32[4,104]{1,0:T(4,128)S(1)}, f32[4,104]{1,0:T(4,128)}, u32[]{:S(2)}) copy-start(f32[4,104]{1,0:T(4,128)} %get-tuple-element.435) | copy-start | bytes 4996 | tf_op jit(solution)/shard_map/while
  313.2 6.0 %copy-start.6 = (s32[16,2,50]{2,1,0:T(2,128)S(1)}, s32[16,2,50]{2,1,0:T(2,128)}, u32[]{:S(2)}) copy-start(s32[16,2,50]{2,1,0:T(2,128)} %copy-done.5) | copy-start | bytes 19204 | tf_op jit(solution)/shard_map/while
  332.5 4.7 %copy-start.9 = (f32[16,104]{1,0:T(8,128)S(1)}, f32[16,104]{1,0:T(8,128)}, u32[]{:S(2)}) copy-start(f32[16,104]{1,0:T(8,128)} %get-tuple-element.434) | copy-start | bytes 19972 | tf_op jit(solution)/shard_map/while
  333.0 4.9 %copy-start.11 = (f32[4,104]{1,0:T(4,128)S(1)}, f32[4,104]{1,0:T(4,128)}, u32[]{:S(2)}) copy-start(f32[4,104]{1,0:T(4,128)} %get-tuple-element.435) | copy-start | bytes 4996 | tf_op jit(solution)/shard_map/while
  333.9 6.1 %copy-start.6 = (s32[16,2,50]{2,1,0:T(2,128)S(1)}, s32[16,2,50]{2,1,0:T(2,128)}, u32[]{:S(2)}) copy-start(s32[16,2,50]{2,1,0:T(2,128)} %copy-done.5) | copy-start | bytes 19204 | tf_op jit(solution)/shard_map/while
  353.4 4.7 %copy-start.9 = (f32[16,104]{1,0:T(8,128)S(1)}, f32[16,104]{1,0:T(8,128)}, u32[]{:S(2)}) copy-start(f32[16,104]{1,0:T(8,128)} %get-tuple-element.434) | copy-start | bytes 19972 | tf_op jit(solution)/shard_map/while
  353.8 4.9 %copy-start.11 = (f32[4,104]{1,0:T(4,128)S(1)}, f32[4,104]{1,0:T(4,128)}, u32[]{:S(2)}) copy-start(f32[4,104]{1,0:T(4,128)} %get-tuple-element.435) | copy-start | bytes 4996 | tf_op jit(solution)/shard_map/while
  354.7 6.1 %copy-start.6 = (s32[16,2,50]{2,1,0:T(2,128)S(1)}, s32[16,2,50]{2,1,0:T(2,128)}, u32[]{:S(2)}) copy-start(s32[16,2,50]{2,1,0:T(2,128)} %copy-done.5) | copy-start | bytes 19204 | tf_op jit(solution)/shard_map/while
  374.2 4.7 %copy-start.9 = (f32[16,104]{1,0:T(8,128)S(1)}, f32[16,104]{1,0:T(8,128)}, u32[]{:S(2)}) copy-start(f32[16,104]{1,0:T(8,128)} %get-tuple-element.434) | copy-start | bytes 19972 | tf_op jit(solution)/shard_map/while
  374.7 4.9 %copy-start.11 = (f32[4,104]{1,0:T(4,128)S(1)}, f32[4,104]{1,0:T(4,128)}, u32[]{:S(2)}) copy-start(f32[4,104]{1,0:T(4,128)} %get-tuple-element.435) | copy-start | bytes 4996 | tf_op jit(solution)/shard_map/while
  375.6 6.1 %copy-start.6 = (s32[16,2,50]{2,1,0:T(2,128)S(1)}, s32[16,2,50]{2,1,0:T(2,128)}, u32[]{:S(2)}) copy-start(s32[16,2,50]{2,1,0:T(2,128)} %copy-done.5) | copy-start | bytes 19204 | tf_op jit(solution)/shard_map/while
  383.5 10.7 %collective-permute-start.6 = (f32[20,12]{0,1:T(8,128)S(1)}, f32[20,12]{0,1:T(8,128)S(1)}, u32[]{:S(2)}, u32[]{:S(2)}) collective-permute-start(f32[20,12]{0,1:T(8,128)S(1)} %bitcast.202), channel_id=1, source_target_pairs={{61,0},{62,1},{63,2},{0,3},{1,4},{2,5},{3,6},{4,7},{5,8},{6,9},{7,... | collective-permute-start | bytes 2888 | tf_op jit(solution)/shard_map/ppermute | solution.py:12
  383.6 12.2 %collective-permute-start.7 = (f32[20,12]{0,1:T(8,128)S(1)}, f32[20,12]{0,1:T(8,128)S(1)}, u32[]{:S(2)}, u32[]{:S(2)}) collective-permute-start(f32[20,12]{0,1:T(8,128)S(1)} %bitcast.201), channel_id=1, source_target_pairs={{62,0},{63,1},{0,2},{1,3},{2,4},{3,5},{4,6},{5,7},{6,8},{7,9},{8,1... | collective-permute-start | bytes 2888 | tf_op jit(solution)/shard_map/ppermute | solution.py:12
  383.7 12.1 %collective-permute-start.8 = (f32[20,12]{0,1:T(8,128)S(1)}, f32[20,12]{0,1:T(8,128)S(1)}, u32[]{:S(2)}, u32[]{:S(2)}) collective-permute-start(f32[20,12]{0,1:T(8,128)S(1)} %bitcast.200), channel_id=1, source_target_pairs={{63,0},{0,1},{1,2},{2,3},{3,4},{4,5},{5,6},{6,7},{7,8},{8,9},{9,10... | collective-permute-start | bytes 2888 | tf_op jit(solution)/shard_map/ppermute | solution.py:12
  386.2 9.6 %collective-permute-start.9 = (f32[20,12]{0,1:T(8,128)S(1)}, f32[20,12]{0,1:T(8,128)S(1)}, u32[]{:S(2)}, u32[]{:S(2)}) collective-permute-start(f32[20,12]{0,1:T(8,128)S(1)} %bitcast.199), channel_id=1, source_target_pairs={{1,0},{2,1},{3,2},{4,3},{5,4},{6,5},{7,6},{8,7},{9,8},{10,9},{11,1... | collective-permute-start | bytes 2888 | tf_op jit(solution)/shard_map/ppermute | solution.py:12
  386.7 9.1 %collective-permute-start.10 = (f32[20,12]{0,1:T(8,128)S(1)}, f32[20,12]{0,1:T(8,128)S(1)}, u32[]{:S(2)}, u32[]{:S(2)}) collective-permute-start(f32[20,12]{0,1:T(8,128)S(1)} %bitcast.197), channel_id=1, source_target_pairs={{2,0},{3,1},{4,2},{5,3},{6,4},{7,5},{8,6},{9,7},{10,8},{11,9},{12,... | collective-permute-start | bytes 2888 | tf_op jit(solution)/shard_map/ppermute | solution.py:12
  394.2 4.7 %collective-permute-start.11 = (f32[20,12]{0,1:T(8,128)S(1)}, f32[20,12]{0,1:T(8,128)S(1)}, u32[]{:S(2)}, u32[]{:S(2)}) collective-permute-start(f32[20,12]{0,1:T(8,128)S(1)} %bitcast.198), channel_id=1, source_target_pairs={{3,0},{4,1},{5,2},{6,3},{7,4},{8,5},{9,6},{10,7},{11,8},{12,9},{13... | collective-permute-start | bytes 2888 | tf_op jit(solution)/shard_map/ppermute | solution.py:12
  (82 other events, 176.1 us)
Sparse Core Ops, SparseCore 0:
  410.6 40.7 all-reduce.1
where the time goes:
time: 464 us; the launch traced here: 460 us
  other arithmetic  133 us (29%)
  local copies, waits for them, and re-layouts  133 us (29%)
  matrix products  89.2 us (19%)
  waiting for transfers between devices  56.5 us (12%)
  starting transfers between devices  22.2 us (5%)
  between operations  14.3 us (3%)
  blocking collectives  8.46 us (2%)
    reduce_sum x16, other arithmetic, pair_weights(): jnp.sum(correlation * correlation * lag_values[None, :], axis=1)  67.3 us
    dot_general x16, matrix products, pair_weights(): jnp.dot(cross_spec.reshape(-1, 2 * freq_count), lag_table, preferred_elem...  61.8 us
    psum x1, waiting for transfers between devices, on_device(): total_normal, total_right = lax.psum((normal_part, right_hand), 'sta')  40.3 us
    dynamic_update_slice x48, local copies, waits for them, and re-layouts, on_device(): lax.scan(one_round, start_acc, round_inputs)  28.6 us
    ppermute x12, starting transfers between devices, shifted(): return lax.ppermute(block, axis, route)  22.1 us
    another operation x17, other arithmetic  19.5 us
    ppermute x12, waiting for transfers between devices, shifted(): return lax.ppermute(block, axis, route)  16.2 us
    dynamic_slice x32, local copies, waits for them, and re-layouts, on_device(): lax.scan(one_round, start_acc, round_inputs)  14.6 us
  transfers between devices with their start and end apart: 13, of which 6 were waited for; matrix products, arithmetic and copies ran while one was open for 2% of the time, Pallas kernels for 0%

commit v1 on v0

v1 whole, which is shorter than its diff:
```python
import functools
import math

import jax
import jax.numpy as jnp
import numpy as np
from jax import lax
from jax.experimental import pallas as pl
from jax.experimental.pallas import tpu as pltpu
from jax.sharding import PartitionSpec as P

F32 = jnp.float32
BF16 = jnp.bfloat16
NT = (((1,), (1,)), ((), ()))
GROUP = 4
PAD_K = 16
MESH = pl.DeviceIdType.MESH


def moment_tables(freq_count):
    n = 2 * freq_count
    f = np.arange(freq_count, dtype=np.float32) * np.float32(math.pi / freq_count)
    lags = np.arange(n - 1, dtype=np.float32) - (freq_count - 1)
    phase = f[:, None] * lags[None, :]
    cosine = np.cos(phase).astype(BF16).astype(np.float64)
    sine = np.sin(phase).astype(BF16).astype(np.float64)
    moment = -2.0 * np.einsum("l,fl,gl->fg", lags.astype(np.float64), cosine, sine)
    w = np.arange(freq_count) * (math.pi / freq_count)
    sign = 1.0 - 2.0 * (np.arange(freq_count) % 2)
    rough = freq_count / 8.0 * w * w
    rough_high = rough.astype(np.float32).astype(BF16).astype(np.float64)
    one = np.zeros((2 * n, 2 * n))
    two = np.zeros((2 * n, n))
    for h in range(2):
        part = slice(h * freq_count, (h + 1) * freq_count)
        later = slice(n + h * freq_count, n + (h + 1) * freq_count)
        one[part, part] = moment
        one[part, n + 4 + h] = sign
        one[h * freq_count, n + 8 + h] = 1.0
        one[later, n + 6 + h] = sign * w
        one[n + h * freq_count, n + 10 + h] = 1.0
        two[part, 0 + h] = freq_count
        two[part, 2 + h] = rough_high
        two[part, 14 + h] = rough - rough_high
        two[later, 12 + h] = 1.0
    ones = np.zeros((16, n))
    ones[0, :freq_count] = 1.0
    ones[1, freq_count:] = 1.0
    order = np.zeros((n, n))
    for k in range(PAD_K * GROUP):
        order[k, (k % GROUP) * PAD_K + k // GROUP] = 1.0
        order[k, n // 2 + (k % GROUP) * PAD_K + k // GROUP] = 1.0
    return [x.astype(np.float32).astype(BF16) for x in (one, two, ones, order)]


def kernel(
    offsets, shape,
    exports_ref, pairs_ref, spec_ref, geo_in_ref, pairs_v_ref, exports_v_ref, mask_ref,
    table_ref, sums_ref, ones_ref, order_ref,
    off_out, side_out,
    spec_send, spec_got, geo_send, geo_got,
    br_ref, bi_ref, bq_ref, en_ref, geo_ref, slot_ref, rbuf, gbuf, off_ref, acc_ref, own_ref,
    side_ref, off_got, side_got,
    spec_ss, spec_rs, geo_ss, geo_rs, off_ss, off_rs, side_ss, side_rs,
):
    events, neighbours, sta_n, clu_n, all_stations = shape
    groups_out = len(offsets)
    capacity = spec_send.shape[1]
    imported = groups_out * capacity
    cands = events + imported
    rows = br_ref.shape[0]
    groups = -(-neighbours // GROUP)
    me_s, me_c = lax.axis_index("sta"), lax.axis_index("clu")
    sta_at = [lax.rem(me_s + d, sta_n) for d in range(sta_n)]
    clu_to = [lax.rem(me_c + o + clu_n, clu_n) for o in offsets] + [me_c]
    clu_back = [lax.rem(me_c - o + clu_n, clu_n) for o in offsets] + [me_c]
    peers = [(d, h) for d in range(sta_n) for h in range(groups_out + 1) if d > 0 or h < groups_out]

    barrier = pltpu.get_barrier_semaphore()
    for d, h in peers:
        pl.semaphore_signal(barrier, inc=1, device_id=(sta_at[d], clu_to[h]), device_id_type=MESH)

    lane8 = lax.broadcasted_iota(jnp.int32, (8, 128), 1) // 32

    def spread_geo(i, c):
        tile = geo_in_ref[i].astype(F32)
        tile = jnp.concatenate([tile, jnp.zeros_like(tile)], axis=1)
        tile = jnp.concatenate([tile, pltpu.roll(tile, 96, 1)], axis=0)
        tile = jnp.where(lane8 == 0, tile, 0.0)
        tile = tile + pltpu.roll(tile, 32, 1)
        geo_ref[i] = tile + pltpu.roll(tile, 64, 1)
        return c

    lax.fori_loop(0, events, spread_geo, 0, unroll=4)

    for h in range(groups_out):
        for c in range(capacity):
            e = exports_ref[h, c]
            spec_send[h, c] = spec_ref[e]
            geo_send[h, c] = geo_ref[e].astype(BF16)

    pl.semaphore_wait(barrier, len(peers))

    def halo(h):
        target = (me_s, clu_to[h])
        return (
            pltpu.make_async_remote_copy(
                src_ref=spec_send.at[h], dst_ref=spec_got.at[h], send_sem=spec_ss.at[h], recv_sem=spec_rs.at[h],
                device_id=target, device_id_type=MESH,
            ),
            pltpu.make_async_remote_copy(
                src_ref=geo_send.at[h], dst_ref=geo_got.at[h], send_sem=geo_ss.at[h], recv_sem=geo_rs.at[h],
                device_id=target, device_id_type=MESH,
            ),
        )

    halos = [copy for h in range(groups_out) for copy in halo(h)]
    for copy in halos:
        copy.start()

    half = 32
    low = lax.broadcasted_iota(jnp.int32, (half, 128), 1) < 64
    ones_rows = ones_ref[...]

    def prepare(tiles, base):
        stacked = []
        for u, tile in enumerate(tiles):
            tile = tile.astype(F32)
            top, bottom = tile[:half], tile[half:]
            real = jnp.where(low, top, pltpu.roll(bottom, 64, 1))
            imag = jnp.where(low, pltpu.roll(top, 64, 1), bottom)
            power = real * real + imag * imag
            br_ref[base + u] = real
            bi_ref[base + u] = imag
            bq_ref[base + u] = power
            stacked.append(power.astype(BF16))
        energy = lax.dot_general(ones_rows, jnp.concatenate(stacked, axis=0), NT, preferred_element_type=F32)[0:8]
        for u in range(GROUP):
            one = jnp.where(lane8 == u, energy, 0.0)
            one = one + pltpu.roll(one, 32, 1)
            en_ref[base + u] = one + pltpu.roll(one, 64, 1)

    def prepare_own(i, c):
        prepare([spec_ref[i * GROUP + u] for u in range(GROUP)], i * GROUP)
        return c

    lax.fori_loop(0, events // GROUP, prepare_own, 0)
    zero_tile = jnp.zeros((half, 128), F32)
    for r in range(cands, rows):
        br_ref[r] = zero_tile
        bi_ref[r] = zero_tile
        bq_ref[r] = zero_tile
        en_ref[r] = jnp.zeros((8, 128), F32)
        geo_ref[r] = jnp.zeros((8, 128), F32)

    rbuf[...] = jnp.zeros_like(rbuf)
    gbuf[...] = jnp.zeros_like(gbuf)
    acc_ref[...] = jnp.zeros_like(acc_ref)
    off_ref[...] = jnp.zeros_like(off_ref)

    pairs_v = pairs_v_ref[...].astype(F32) + 1.0
    pairs_v = jnp.concatenate([pairs_v, jnp.zeros((events, 128 - neighbours), F32)], axis=1).astype(BF16)
    slot_ref[...] = jnp.dot(pairs_v, order_ref[...], preferred_element_type=F32) - 1.0

    lane16 = lax.broadcasted_iota(jnp.int32, (16, 128), 1) // 32
    block_mask = [jnp.where(lane16 == u, 1.0, 0.0).astype(BF16) for u in range(GROUP)]
    cand_iota = lax.broadcasted_iota(jnp.int32, (cands, 128), 0).astype(F32)
    row_e = lax.broadcasted_iota(jnp.int32, (128, 128), 0) // 32 * 32
    col_e = lax.broadcasted_iota(jnp.int32, (128, 128), 1)
    table = table_ref[...]
    sums = sums_ref[...]

    def pick4(parts, lanes):
        return jnp.where(
            lanes < 2, jnp.where(lanes == 0, parts[0], parts[1]), jnp.where(lanes == 2, parts[2], parts[3])
        )

    for copy in halos:
        copy.wait()

    def prepare_got(h):
        for i in range(capacity // GROUP):
            base = events + h * capacity + i * GROUP
            prepare([spec_got[h, i * GROUP + u] for u in range(GROUP)], base)
            for u in range(GROUP):
                geo_ref[base + u] = geo_got[h, i * GROUP + u].astype(F32)

    def prepare_step(h, c):
        prepare_got(h)
        return c

    lax.fori_loop(0, groups_out, prepare_step, 0)

    def one_event(e, carry):
        ar, ai, aq = br_ref[e], bi_ref[e], bq_ref[e]
        ids = []
        for k in range(groups * GROUP):
            if k < neighbours:
                c = pairs_ref[e, k]
                ids.append(jnp.where(c < 0, cands, c))
            else:
                ids.append(cands)
        xr_all, xi_all, q_all = [], [], []
        for c in ids:
            br, bi = br_ref[c], bi_ref[c]
            xr_all.append((ar * br + ai * bi).astype(BF16))
            xi_all.append((ai * br - ar * bi).astype(BF16))
            q_all.append((aq * bq_ref[c]).astype(BF16))
        xr = jnp.concatenate(xr_all, axis=0)
        xi = jnp.concatenate(xi_all, axis=0)
        q = jnp.concatenate(q_all, axis=0)
        y = jnp.dot(jnp.concatenate([xr, xi], axis=1), table, preferred_element_type=F32)
        z = (y[:, :128] * xi.astype(F32)).astype(BF16)
        t = jnp.dot(jnp.concatenate([q, z], axis=1), sums, preferred_element_type=F32) + y[:, 128:]
        for kg in range(groups):
            four = ids[kg * GROUP : (kg + 1) * GROUP]
            rbuf[pl.ds(kg * 16, 16), :] = t[kg * 128 : (kg + 1) * 128].T[:16]
            gbuf[pl.ds(kg * 16, 8), :] = pick4([geo_ref[c] for c in four], lane8)
            gbuf[pl.ds(kg * 16 + 8, 8), :] = pick4([en_ref[c] for c in four], lane8)

        masks = []
        for u in range(GROUP):
            count = len(range(u, neighbours, GROUP))
            part = mask_ref[e, pl.ds(u, count, stride=GROUP), :].astype(F32) * (1.0 / all_stations)
            part = jnp.concatenate([part, jnp.zeros((PAD_K - count, part.shape[1]), F32)], axis=0)
            masks.append(jnp.concatenate([part, jnp.zeros_like(part)], axis=1))
        live = []
        for h in range(2):
            parts = []
            for u in range(GROUP):
                shift = (32 * u - 32 * h) % 128
                parts.append(pltpu.roll(masks[u], shift, 1) if shift else masks[u])
            live.append(pick4(parts, lane16))

        def quantity(ref, r):
            return ref[pl.ds(r, PAD_K, stride=16), :]

        ga = geo_ref[e]
        ea = en_ref[e]
        weighted, moved, offs = [], [], [None] * 16
        for h in range(2):
            first = quantity(rbuf, 8 + h)
            first_i = quantity(rbuf, 10 + h)
            alt = quantity(rbuf, 4 + h)
            alt_i = quantity(rbuf, 6 + h)
            power = quantity(rbuf, h) + 64.0 * (first * first - first_i * first_i) - alt * alt
            rough8 = quantity(rbuf, 2 + h) + quantity(rbuf, 14 + h) - 0.125 * (alt_i * alt_i)
            small = 1e-6 * (ea[h : h + 1] * quantity(gbuf, 8 + h) + 1e-6)
            weight = live[h] * power / (power + rough8 + small)
            delayed = weight * quantity(rbuf, 12 + h) / (power + small)
            weighted.append(weight)
            moved.append(delayed)
            gb = [quantity(gbuf, 4 * h + j) for j in range(4)]
            for i in range(4):
                wi = weight * ga[4 * h + i : 4 * h + i + 1]
                for j in range(4):
                    term = wi * gb[j]
                    offs[4 * i + j] = term if h == 0 else offs[4 * i + j] + term
        place = jnp.where(col_e == row_e + e, -1.0, 0.0).astype(BF16)
        offs = jnp.concatenate(offs, axis=0)
        off_ref[...] += jnp.dot(offs.astype(BF16), place, preferred_element_type=F32)

        columns = []
        for n, value in enumerate(weighted + moved):
            own_ref[n, pl.ds(e, 1), :] = jnp.sum(value, axis=0, keepdims=True)
            value_high = value.astype(BF16)
            value_low = (value - value_high.astype(F32)).astype(BF16)
            columns.append(
                jnp.concatenate([v * m for v in (value_high, value_low) for m in block_mask], axis=0)
            )
        columns = jnp.concatenate(columns, axis=1)
        hot = jnp.where(cand_iota == slot_ref[pl.ds(e, 1), :], 1.0, 0.0).astype(BF16)
        acc_ref[...] += jnp.dot(hot, columns, preferred_element_type=F32)
        return carry

    lax.fori_loop(0, events, one_event, 0)

    share = off_ref.shape[0] // sta_n

    def off_copy(d):
        return pltpu.make_async_remote_copy(
            src_ref=off_ref.at[pl.ds(sta_at[d] * share, share)], dst_ref=off_got.at[d - 1],
            send_sem=off_ss.at[d - 1], recv_sem=off_rs.at[d - 1],
            device_id=(sta_at[d], me_c), device_id_type=MESH,
        )

    off_copies = [off_copy(d) for d in range(1, sta_n)]
    for copy in off_copies:
        copy.start()

    lane_out = lax.broadcasted_iota(jnp.int32, (cands, 128), 1)
    pad = jnp.zeros((imported, 128), F32)
    totals = []
    for n in range(4):
        own = jnp.concatenate([own_ref[n], pad], axis=0)
        part = acc_ref[:, n * 128 : (n + 1) * 128]
        totals.append(part + own if n < 2 else own - part)

    result = jnp.zeros((cands, 128), F32)
    geo_t = geo_ref.reshape(rows * 8, 128)
    geos = [geo_t[pl.ds(n, cands, stride=8), :] for n in range(8)]
    for i in range(4):
        scaled = [totals[h] * geos[4 * h + i] for h in range(2)]
        for j in range(i, 4):
            value = jnp.sum(scaled[0] * geos[j] + scaled[1] * geos[4 + j], axis=1, keepdims=True)
            keep = (lane_out == 8 * i + j) | (lane_out == 8 * j + i)
            result = jnp.where(keep, value, result)
        value = jnp.sum(totals[2] * geos[i] + totals[3] * geos[4 + i], axis=1, keepdims=True)
        result = jnp.where(lane_out == 8 * i + 4, value, result)
    result = jnp.concatenate([result, jnp.zeros((128 - cands, 128), F32)], axis=0).T
    for x in range(sta_n):
        side_ref[x] = result[8 * x : 8 * x + 8]

    def side_copy(n):
        d, h = peers[n]
        return pltpu.make_async_remote_copy(
            src_ref=side_ref.at[sta_at[d]], dst_ref=side_got.at[n],
            send_sem=side_ss.at[n], recv_sem=side_rs.at[n],
            device_id=(sta_at[d], clu_back[h]), device_id_type=MESH,
        )

    side_copies = [side_copy(n) for n in range(len(peers))]
    for copy in side_copies:
        copy.start()
    for copy in off_copies:
        copy.wait()
    total = off_ref[pl.ds(me_s * share, share), :]
    for d in range(1, sta_n):
        total = total + off_got[d - 1]
    off_out[...] = total
    for copy in side_copies:
        copy.wait()

    kept = side_ref[me_s]
    for n, (d, h) in enumerate(peers):
        if h == groups_out:
            kept = kept + side_got[n]
    lane_c = lax.broadcasted_iota(jnp.int32, (8, 128), 1)
    away = jnp.zeros((8, 128), F32)
    for h in range(groups_out):
        part = jnp.zeros((8, 128), F32)
        for n, (d, g) in enumerate(peers):
            if g == h:
                part = part + side_got[n]
        lowest = events + h * capacity
        away = jnp.where((lane_c >= lowest) & (lane_c < lowest + capacity), part, away)
    owner = jnp.where(
        lax.broadcasted_iota(jnp.int32, (events, 128), 0) == exports_v_ref[...], 1.0, 0.0
    ).astype(BF16)
    back = jnp.zeros((8, events), F32)
    for _ in range(3):
        piece = away.astype(BF16)
        back = back + lax.dot_general(piece, owner, NT, preferred_element_type=F32)
        away = away - piece.astype(F32)
    side_out[...] = kept[:, :events] + back


def on_device(spectra, partials, pair_list, station_mask, exports):
    events, stations, two_freq = spectra.shape
    sta_n, clu_n = lax.axis_size("sta"), lax.axis_size("clu")
    groups_out, capacity = exports.shape
    half_span = groups_out // 2
    neighbours = pair_list.shape[1]
    imported = groups_out * capacity
    cands = events + imported
    rows = cands + 1
    offsets = [h - half_span + (1 if h >= half_span else 0) for h in range(groups_out)]
    n_peers = sta_n * (groups_out + 1) - 1
    exports_v = jnp.pad(exports.reshape(1, -1), ((0, 0), (events, 128 - cands)), constant_values=-1)
    smem = pl.BlockSpec(memory_space=pltpu.SMEM)
    vmem = pl.BlockSpec(memory_space=pltpu.VMEM)
    dma = pltpu.SemaphoreType.DMA
    share = 16 * PAD_K // sta_n
    off, side = pl.pallas_call(
        functools.partial(kernel, offsets, (events, neighbours, sta_n, clu_n, stations * sta_n)),
        out_shape=(jax.ShapeDtypeStruct((share, 128), F32), jax.ShapeDtypeStruct((8, events), F32)),
        in_specs=[smem, smem] + [vmem] * 9,
        out_specs=(vmem, vmem),
        scratch_shapes=[
            pltpu.VMEM((groups_out, capacity, stations, two_freq), BF16),
            pltpu.VMEM((groups_out, capacity, stations, two_freq), BF16),
            pltpu.VMEM((groups_out, capacity, 8, 128), BF16),
            pltpu.VMEM((groups_out, capacity, 8, 128), BF16),
            pltpu.VMEM((rows, 32, 128), F32),
            pltpu.VMEM((rows, 32, 128), F32),
            pltpu.VMEM((rows, 32, 128), F32),
            pltpu.VMEM((rows, 8, 128), F32),
            pltpu.VMEM((rows, 8, 128), F32),
            pltpu.VMEM((events, 128), F32),
            pltpu.VMEM((PAD_K * 16, 128), F32),
            pltpu.VMEM((PAD_K * 16, 128), F32),
            pltpu.VMEM((16 * PAD_K, 128), F32),
            pltpu.VMEM((cands, 512), F32),
            pltpu.VMEM((4, events, 128), F32),
            pltpu.VMEM((sta_n, 8, 128), F32),
            pltpu.VMEM((sta_n - 1, share, 128), F32),
            pltpu.VMEM((n_peers, 8, 128), F32),
            dma((groups_out,)), dma((groups_out,)), dma((groups_out,)), dma((groups_out,)),
            dma((sta_n - 1,)), dma((sta_n - 1,)), dma((n_peers,)), dma((n_peers,)),
        ],
        compiler_params=pltpu.CompilerParams(
            vmem_limit_bytes=48 << 20, collective_id=0, has_side_effects=True
        ),
    )(
        exports, pair_list, spectra, partials, pair_list, exports_v, station_mask,
        *[jnp.asarray(x) for x in moment_tables(two_freq // 2)],
    )
    off = off.reshape(16 // sta_n, PAD_K * GROUP, events)[:, :neighbours]
    normal = jnp.concatenate([side[: 16 // sta_n, None, :], off], axis=1)
    return (normal, side[4:5])


def solution(mesh):
    return jax.shard_map(
        on_device,
        mesh=mesh,
        in_specs=(
            P("clu", "sta", None),
            P("clu", None, "sta"),
            P("clu", None),
            P("clu", None, "sta"),
            P("clu", None),
        ),
        out_specs=(P("sta", None, "clu"), P("sta", "clu")),
        check_vma=False,
    )
```

time: 464 us -> 76.2 us (0.16)
  other arithmetic: 133 us -> 0.02 us
  local copies, waits for them, and re-layouts: 133 us -> 3.9 us
  matrix products: 89.2 us -> 0 us
  Pallas kernels: 0 us -> 71.3 us
  waiting for transfers between devices: 56.5 us -> 0 us
  starting transfers between devices: 22.2 us -> 0 us
  between operations: 14.3 us -> 0.76 us
  blocking collectives: 8.46 us -> 0 us
    dot_general x114 -> x0, matrix products: 89.2 us -> none  [the longest x16 61.8 us: pair_weights(): jnp.dot(cross_spec.reshape(-1, 2 * freq_count), lag_table, preferred_elem...]
    reduce_sum x50 -> x0, other arithmetic: 75.2 us -> none  [the longest x16 67.3 us: pair_weights(): jnp.sum(correlation * correlation * lag_values[None, :], axis=1)]
    pallas_call x0 -> x1, Pallas kernels: none -> 71.3 us  [on_device(): pl.pallas_call(functools.partial(kernel, offsets, (events, neighbours, st...]
    gather x82 -> x0, local copies, waits for them, and re-layouts: 40.5 us -> none  [the longest x16 13.8 us: one_round(): cand_spec[partner_b]]
    psum x1 -> x0, waiting for transfers between devices: 40.3 us -> none  [on_device(): total_normal, total_right = lax.psum((normal_part, right_hand), 'sta')]
    dynamic_update_slice x48 -> x0, local copies, waits for them, and re-layouts: 28.6 us -> none  [on_device(): lax.scan(one_round, start_acc, round_inputs)]
    ppermute x12 -> x0, starting transfers between devices: 22.1 us -> none  [shifted(): return lax.ppermute(block, axis, route)]
    another operation x17 -> x0, other arithmetic: 19.5 us -> none
  transfers between devices with their start and end apart: 13 -> 0, of which waited for: 6 -> 0; matrix products, arithmetic and copies ran while one was open for 2% -> 0% of each run, Pallas kernels for 0% -> 0%
where the time goes in v1:
time: 76.2 us; the launch traced here: 76 us
  Pallas kernels  71.3 us (94%)
  local copies, waits for them, and re-layouts  3.9 us (5%)
    pallas_call x1, Pallas kernels, on_device(): pl.pallas_call(functools.partial(kernel, offsets, (events, neighbours, st...  71.3 us
    unnamed x18, local copies, waits for them, and re-layouts  2.46 us

profile of v1, /device:TPU:1, one launch (start us, length us, event | category | flops | bytes accessed | tf_op | source)
XLA Modules:
  0.0 76.0 jit_solution(11622962051489299477)
XLA Ops:
  0.6 0.8 %reshape.10 = s32[1,72]{1,0:T(1,128)S(1)} reshape(s32[6,12]{1,0:T(8,128)} %exports_ref.1) | data formatting | bytes 576 | tf_op jit(solution)/shard_map/reshape | solution.py:369
  1.4 0.1 pad.4.exports_v_ref
  1.5 0.0 copy-start
  1.5 0.0 copy-start.1
  1.5 0.0 copy-start.2
  1.5 0.0 copy-start.3
  1.5 0.0 copy-start.4
  1.5 0.0 copy-start.5
  1.5 0.0 copy-start.6
  1.5 0.0 copy-start.7
  1.5 1.7 %copy.14.mask_ref = s32[32,50,64]{2,1,0:T(8,128)S(1)} copy(s32[32,50,64]{2,0,1:T(8,128)} %param.12) | data formatting | bytes 819200 | tf_op args[3]
  3.2 0.0 copy-done
  3.2 0.0 copy-done.1
  3.2 0.0 copy-done.2
  3.2 0.0 copy-done.3
  3.3 0.0 copy-done.4
  3.3 0.0 copy-done.5
  3.3 0.0 copy-done.6
  3.3 0.0 copy-done.7
  3.3 71.3 %shard_map.104 = (f32[64,128]{1,0:T(8,128)S(1)}, f32[8,32]{1,0:T(8,128)S(1)}) custom-call(s32[6,12]{1,0:T(8,128)S(1)} %copy-done.6, s32[32,50]{1,0:T(8,128)S(1)} %copy-done.2, bf16[32,64,128]{2,1,0:T(8,128)(2,1)S(1)} %copy-done, bf16[32,4,64]{2,1,0:T(4,128)(2,1)S(1)} %copy-done.4, s32[32,50]{1,0:T(8,128)S(1)} %copy-done.2, s32[1,128]{1,0:T(1,128)S(1)} %pad.4.exports_v_ref, ...), custom_call_target="tpu_custom_call" | custom-call | tf_op jit(solution)/shard_map/pallas_call | solution.py:374
  74.6 0.5 slice.11
  75.2 0.1 reshape.11
  75.3 0.7 copy.16
  (3 shorter events, 0.0 us)
Async XLA Ops:
  1.5 1.7 %copy-start = (bf16[32,64,128]{2,1,0:T(8,128)(2,1)S(1)}, bf16[32,64,128]{2,1,0:T(8,128)(2,1)}, u32[]{:S(2)}) copy-start(bf16[32,64,128]{2,1,0:T(8,128)(2,1)} %spec_ref.1) | copy-start | bytes 1572868
  1.5 1.8 %copy-start.1 = (bf16[256,256]{1,0:T(8,128)(2,1)S(1)}, bf16[256,256]{1,0:T(8,128)(2,1)}, u32[]{:S(2)}) copy-start(bf16[256,256]{1,0:T(8,128)(2,1)} %constant.10.clone.table_ref) | copy-start | bytes 393220
  1.5 1.8 %copy-start.2 = (s32[32,50]{1,0:T(8,128)S(1)}, s32[32,50]{1,0:T(8,128)}, u32[]{:S(2)}) copy-start(s32[32,50]{1,0:T(8,128)} %pairs_v_ref.1) | copy-start | bytes 19204
  1.5 1.8 %copy-start.3 = (bf16[256,128]{1,0:T(8,128)(2,1)S(1)}, bf16[256,128]{1,0:T(8,128)(2,1)}, u32[]{:S(2)}) copy-start(bf16[256,128]{1,0:T(8,128)(2,1)} %constant.11.clone.sums_ref) | copy-start | bytes 196612
  1.5 1.8 %copy-start.4 = (bf16[32,4,64]{2,1,0:T(4,128)(2,1)S(1)}, bf16[32,4,64]{2,1,0:T(4,128)(2,1)}, u32[]{:S(2)}) copy-start(bf16[32,4,64]{2,1,0:T(4,128)(2,1)} %geo_in_ref.1) | copy-start | bytes 49156
  1.5 1.8 %copy-start.5 = (bf16[128,128]{1,0:T(8,128)(2,1)S(1)}, bf16[128,128]{1,0:T(8,128)(2,1)}, u32[]{:S(2)}) copy-start(bf16[128,128]{1,0:T(8,128)(2,1)} %constant.13.clone.order_ref) | copy-start | bytes 98308
  1.5 1.8 %copy-start.6 = (s32[6,12]{1,0:T(8,128)S(1)}, s32[6,12]{1,0:T(8,128)}, u32[]{:S(2)}) copy-start(s32[6,12]{1,0:T(8,128)} %exports_ref.1) | copy-start | bytes 868
  1.5 1.8 %copy-start.7 = (bf16[16,128]{1,0:T(8,128)(2,1)S(1)}, bf16[16,128]{1,0:T(8,128)(2,1)}, u32[]{:S(2)}) copy-start(bf16[16,128]{1,0:T(8,128)(2,1)} %constant.12.clone.ones_ref) | copy-start | bytes 12292

commit v2 on v1

v2 whole, which is shorter than its diff:
```python
import functools
import math

import jax
import jax.numpy as jnp
import numpy as np
from jax import lax
from jax.experimental import pallas as pl
from jax.experimental.pallas import tpu as pltpu
from jax.sharding import PartitionSpec as P

F32 = jnp.float32
BF16 = jnp.bfloat16
NT = (((1,), (1,)), ((), ()))
CHUNKS = 2
GROUP = 8
PAD_K = 8
REP = 16
MESH = pl.DeviceIdType.MESH


def moment_tables(freq_count):
    n = 2 * freq_count
    f = np.arange(freq_count, dtype=np.float32) * np.float32(math.pi / freq_count)
    lags = np.arange(n - 1, dtype=np.float32) - (freq_count - 1)
    phase = f[:, None] * lags[None, :]
    cosine = np.cos(phase).astype(BF16).astype(np.float64)
    sine = np.sin(phase).astype(BF16).astype(np.float64)
    moment = -2.0 * np.einsum("l,fl,gl->fg", lags.astype(np.float64), cosine, sine)
    w = np.arange(freq_count) * (math.pi / freq_count)
    sign = 1.0 - 2.0 * (np.arange(freq_count) % 2)
    rough = freq_count / 8.0 * w * w
    rough_high = rough.astype(np.float32).astype(BF16).astype(np.float64)
    one = np.zeros((2 * n, 2 * n))
    two = np.zeros((2 * n, n))
    for h in range(2):
        part = slice(h * freq_count, (h + 1) * freq_count)
        later = slice(n + h * freq_count, n + (h + 1) * freq_count)
        one[part, part] = moment
        one[part, n + 4 + h] = sign
        one[h * freq_count, n + 8 + h] = 1.0
        one[later, n + 6 + h] = sign * w
        one[n + h * freq_count, n + 10 + h] = 1.0
        two[part, 0 + h] = freq_count
        two[part, 2 + h] = rough_high
        two[part, 14 + h] = rough - rough_high
        two[later, 12 + h] = 1.0
    ones = np.zeros((16, n))
    ones[0, :freq_count] = 1.0
    ones[1, freq_count:] = 1.0
    order = np.zeros((n, n))
    for k in range(PAD_K * GROUP):
        order[k, (k % GROUP) * PAD_K + k // GROUP] = 1.0
        order[k, GROUP * PAD_K + (k % GROUP) * PAD_K + k // GROUP] = 1.0
    both = np.zeros((2 * n, 5 * n))
    both[:, : 2 * n] = one
    both[:, 2 * n : 3 * n] = two
    both[:n, 3 * n : 4 * n] = order
    both[:16, 4 * n :] = ones
    return both.astype(np.float32).astype(BF16)


def kernel(
    offsets, shape,
    exports_ref, pairs_ref, spec_hbm, geo_hbm, pairs_hbm, exports_hbm, mask_hbm, consts_hbm,
    off_out, right_out,
    spec_ref, geo_in_ref, pairs_v_ref, exports_v_ref, mask_ref, consts_ref, exports_row, load_sems,
    spec_send, spec_got, geo_send, geo_got,
    br_ref, bi_ref, bq_ref, en_ref, geo_ref, slot_ref, off_ref, acc_ref, own_ref,
    side_ref, off_got, side_got, last_ref,
    cross_a, cross_b, quad_a, quad_b, rbuf_a, rbuf_b, gbuf_a, gbuf_b, live_ref, hot_ref, place_ref,
    spec_ss, spec_rs, geo_ss, geo_rs, off_ss, off_rs, side_ss, side_rs,
):
    events, neighbours, sta_n, clu_n, all_stations = shape
    groups_out = len(offsets)
    capacity = geo_send.shape[1]
    imported = groups_out * capacity
    cands = events + imported
    rows = geo_ref.shape[0]
    me_s, me_c = lax.axis_index("sta"), lax.axis_index("clu")
    sta_at = [lax.rem(me_s + d, sta_n) for d in range(sta_n)]
    clu_to = [lax.rem(me_c + o + clu_n, clu_n) for o in offsets] + [me_c]
    clu_back = [lax.rem(me_c - o + clu_n, clu_n) for o in offsets] + [me_c]
    peers = [(d, h) for d in range(sta_n) for h in range(groups_out + 1) if d > 0 or h < groups_out]

    loads = [
        pltpu.make_async_copy(source, target, load_sems.at[n])
        for n, (source, target) in enumerate((
            (spec_hbm, spec_ref), (geo_hbm, geo_in_ref), (consts_hbm, consts_ref), (exports_hbm, exports_v_ref),
            (pairs_hbm, pairs_v_ref), (mask_hbm, mask_ref),
        ))
    ]
    for copy in loads:
        copy.start()
    barrier = pltpu.get_barrier_semaphore()
    for d, h in peers:
        pl.semaphore_signal(barrier, inc=1, device_id=(sta_at[d], clu_to[h]), device_id_type=MESH)

    loads[0].wait()
    loads[1].wait()
    for h in range(groups_out):
        for c in range(capacity):
            e = exports_ref[h, c]
            tile = spec_ref[e]
            for ch in range(CHUNKS):
                spec_send[ch, h, c] = jnp.concatenate(
                    [tile[REP * ch : REP * (ch + 1)], tile[32 + REP * ch : 32 + REP * (ch + 1)]], axis=0
                )
            geo_send[h, c] = geo_in_ref[e]

    pl.semaphore_wait(barrier, len(peers))

    def halo(ch, h):
        return pltpu.make_async_remote_copy(
            src_ref=spec_send.at[ch, h], dst_ref=spec_got.at[ch, h],
            send_sem=spec_ss.at[ch, h], recv_sem=spec_rs.at[ch, h],
            device_id=(me_s, clu_to[h]), device_id_type=MESH,
        )

    def geo_halo(h):
        return pltpu.make_async_remote_copy(
            src_ref=geo_send.at[h], dst_ref=geo_got.at[h], send_sem=geo_ss.at[h], recv_sem=geo_rs.at[h],
            device_id=(me_s, clu_to[h]), device_id_type=MESH,
        )

    order_h = sorted(range(groups_out), key=lambda h: -abs(offsets[h]))
    geo_halos = [geo_halo(h) for h in order_h]
    halos = [[halo(ch, h) for h in order_h] for ch in range(CHUNKS)]
    for copy in geo_halos + sum(halos, []):
        copy.start()

    block8 = lax.broadcasted_iota(jnp.int32, (8, 128), 1) // REP
    lane8 = lax.broadcasted_iota(jnp.int32, (8, 128), 1)
    low = lax.broadcasted_iota(jnp.int32, (REP, 128), 1) < 64
    for copy in loads[2:]:
        copy.wait()
    ones_rows = consts_ref[0:16, 512:640]

    def repeat(tile):
        tile = tile + pltpu.roll(tile, 16, 1)
        tile = tile + pltpu.roll(tile, 32, 1)
        return tile + pltpu.roll(tile, 64, 1)

    def spread_geo(tile, c):
        tile = tile.astype(F32)
        tile = jnp.concatenate([tile, jnp.zeros_like(tile)], axis=1)
        for ch in range(CHUNKS):
            first = pltpu.roll(tile, 128 - REP * ch, 1) if ch else tile
            both = jnp.concatenate([first, pltpu.roll(tile, 128 - 32 - REP * ch, 1)], axis=0)
            geo_ref[c, 8 * ch : 8 * ch + 8] = repeat(jnp.where(block8 == 0, both, 0.0))

    def prepare(ch, tiles, base):
        stacked = []
        for u, (top, bottom) in enumerate(tiles):
            top, bottom = top.astype(F32), bottom.astype(F32)
            real = jnp.where(low, top, pltpu.roll(bottom, 64, 1))
            imag = jnp.where(low, pltpu.roll(top, 64, 1), bottom)
            power = real * real + imag * imag
            br_ref[ch, base + u] = real
            bi_ref[ch, base + u] = imag
            bq_ref[ch, base + u] = power
            stacked.append(power)
        stacked = jnp.concatenate(stacked, axis=0).astype(BF16)
        energy = lax.dot_general(ones_rows, stacked, NT, preferred_element_type=F32)[0:8]
        for u in range(GROUP):
            en_ref[ch, base + u] = repeat(jnp.where(block8 == u, energy, 0.0))

    def prepare_own(i, c):
        for ch in range(CHUNKS):
            tiles = []
            for u in range(GROUP):
                tile = spec_ref[i * GROUP + u]
                tiles.append((tile[REP * ch : REP * (ch + 1)], tile[32 + REP * ch : 32 + REP * (ch + 1)]))
            prepare(ch, tiles, i * GROUP)
        for u in range(GROUP):
            spread_geo(geo_in_ref[i * GROUP + u], i * GROUP + u)
        return c

    lax.fori_loop(0, events // GROUP, prepare_own, 0)
    for r in range(cands, rows):
        for ch in range(CHUNKS):
            br_ref[ch, r] = jnp.zeros((REP, 128), F32)
            bi_ref[ch, r] = jnp.zeros((REP, 128), F32)
            bq_ref[ch, r] = jnp.zeros((REP, 128), F32)
            en_ref[ch, r] = jnp.zeros((8, 128), F32)
        geo_ref[r] = jnp.zeros((8 * CHUNKS, 128), F32)

    for ref in (acc_ref, off_ref, rbuf_a, rbuf_b, gbuf_a, gbuf_b, last_ref):
        ref[...] = jnp.zeros_like(ref)

    exports_row[...] = jnp.full_like(exports_row, -1)
    exports_row[0:groups_out, 0:capacity] = exports_v_ref[...]
    pairs_v = pairs_v_ref[...].astype(F32) + 1.0
    pairs_v = jnp.concatenate([pairs_v, jnp.zeros((events, 128 - neighbours), F32)], axis=1).astype(BF16)
    slot_ref[...] = jnp.dot(pairs_v, consts_ref[0:128, 384:512], preferred_element_type=F32) - 1.0

    cand_iota = lax.broadcasted_iota(jnp.int32, (cands, 128), 0).astype(F32)
    row_e = lax.broadcasted_iota(jnp.int32, (128, 256), 0) // REP * 32
    col_e = lax.broadcasted_iota(jnp.int32, (128, 256), 1)
    table = consts_ref[:, 0:256]
    sums = consts_ref[:, 256:384]

    def pick(parts, base=0):
        if len(parts) == 1:
            return parts[0]
        mid = len(parts) // 2
        return jnp.where(block8 < base + mid, pick(parts[:mid], base), pick(parts[mid:], base + mid))

    def slot_ids(e):
        ids = []
        for k in range(neighbours):
            c = pairs_ref[e, k]
            ids.append(jnp.where(c < 0, cands, c))
        return ids

    def stage_a(ch, pair, cross, quad):
        for v in range(2):
            e = 2 * pair + v
            ar, ai, aq = br_ref[ch, e], bi_ref[ch, e], bq_ref[ch, e]
            for k, c in enumerate(slot_ids(e)):
                br, bi = br_ref[ch, c], bi_ref[ch, c]
                at = pl.ds((v * neighbours + k) * REP, REP)
                cross[at, 0:128] = (ar * br + ai * bi).astype(BF16)
                cross[at, 128:256] = (ai * br - ar * bi).astype(BF16)
                quad[at, :] = (aq * bq_ref[ch, c]).astype(BF16)

    def stage_b(ch, pair, cross, quad, rbuf, gbuf):
        y = jnp.dot(cross[...], table, preferred_element_type=F32)
        z = (y[:, :128] * cross[:, 128:256].astype(F32)).astype(BF16)
        t = jnp.dot(jnp.concatenate([quad[...], z], axis=1), sums, preferred_element_type=F32) + y[:, 128:]
        for v in range(2):
            ids = slot_ids(2 * pair + v)
            for kg in range(-(-neighbours // GROUP)):
                first = v * neighbours * REP + kg * 128
                last = min(first + 128, (v + 1) * neighbours * REP)
                part = t[first:last]
                if part.shape[0] < 128:
                    part = jnp.concatenate([part, jnp.zeros((128 - part.shape[0], 128), F32)], axis=0)
                rbuf[v, pl.ds(kg * 16, 16), :] = part.T[:16]
                some = ids[kg * GROUP : (kg + 1) * GROUP]
                some = some + [cands] * (GROUP - len(some))
                gbuf[v, pl.ds(kg * 16, 8), :] = pick([geo_ref[c, 8 * ch : 8 * ch + 8] for c in some])
                gbuf[v, pl.ds(kg * 16 + 8, 8), :] = pick([en_ref[ch, c] for c in some])

    def make_live(e):
        masks = []
        for u in range(GROUP):
            count = len(range(u, neighbours, GROUP))
            part = mask_ref[pl.ds(u * events + e, count, stride=GROUP * events), :].astype(F32)
            part = jnp.concatenate([part, jnp.zeros((PAD_K - count, part.shape[1]), F32)], axis=0)
            masks.append(jnp.concatenate([part, jnp.zeros_like(part)], axis=1))
        for ch in range(CHUNKS):
            for h in range(2):
                parts = []
                for u in range(GROUP):
                    shift = (REP * u - 32 * h - REP * ch) % 128
                    parts.append(pltpu.roll(masks[u], shift, 1) if shift else masks[u])
                live_ref[ch, e, 8 * h : 8 * h + 8] = pick(parts) * (1.0 / all_stations)

    def make_pair(pair, c):
        lanes = lax.broadcasted_iota(jnp.int32, (1, 128), 1)
        slots = jnp.where(lanes < 64, slot_ref[pl.ds(2 * pair, 1), :], slot_ref[pl.ds(2 * pair + 1, 1), :])
        hot_ref[pair] = jnp.where(cand_iota == slots, 1.0, 0.0).astype(BF16)
        for v in range(2):
            make_live(2 * pair + v)
            place = jnp.where(col_e == row_e + (2 * pair + v), -1.0, 0.0).astype(BF16)
            place_ref[pair, 128 * v : 128 * v + 128] = place
        return c

    lax.fori_loop(0, events // 2, make_pair, 0)

    def stage_c(ch, pair, rbuf, gbuf):
        offs_pair, column_pair = [], []
        for v in range(2):
            e = 2 * pair + v

            def quantity(ref, r, v=v):
                return ref[v, pl.ds(r, PAD_K, stride=16), :]

            live = live_ref[ch, e]
            ga = geo_ref[e, 8 * ch : 8 * ch + 8]
            ea = en_ref[ch, e]
            weighted, moved, offs = [], [], [None] * 16
            for h in range(2):
                first = quantity(rbuf, 8 + h)
                first_i = quantity(rbuf, 10 + h)
                alt = quantity(rbuf, 4 + h)
                alt_i = quantity(rbuf, 6 + h)
                power = quantity(rbuf, h) + 64.0 * (first * first - first_i * first_i) - alt * alt
                rough8 = quantity(rbuf, 2 + h) + quantity(rbuf, 14 + h) - 0.125 * (alt_i * alt_i)
                small = 1e-6 * (ea[h : h + 1] * quantity(gbuf, 8 + h) + 1e-6)
                weight = live[8 * h : 8 * h + 8] * power / (power + rough8 + small)
                delayed = weight * quantity(rbuf, 12 + h) / (power + small)
                weighted.append(weight)
                moved.append(delayed)
                gb = [quantity(gbuf, 4 * h + j) for j in range(4)]
                for i in range(4):
                    wi = weight * ga[4 * h + i : 4 * h + i + 1]
                    for j in range(4):
                        term = wi * gb[j]
                        offs[4 * i + j] = term if h == 0 else offs[4 * i + j] + term
            offs_pair.append(jnp.concatenate(offs, axis=0))
            columns = []
            for n, value in enumerate(weighted + moved):
                own_ref[ch, n, pl.ds(e, 1), :] = jnp.sum(value, axis=0, keepdims=True)
                columns.append(
                    jnp.concatenate([jnp.where(block8 == u, value, 0.0) for u in range(GROUP)], axis=0)
                )
            column_pair.append(jnp.concatenate(columns, axis=1))
        offs = jnp.concatenate(offs_pair, axis=1).astype(BF16)
        off_ref[...] += jnp.dot(offs, place_ref[pair], preferred_element_type=F32)
        columns = jnp.concatenate(column_pair, axis=0).astype(BF16)
        acc_ref[ch] += jnp.dot(hot_ref[pair], columns, preferred_element_type=F32)

    for copy in geo_halos:
        copy.wait()

    def spread_got(h, c):
        for i in range(capacity):
            spread_geo(geo_got[h, i], events + h * capacity + i)
        return c

    lax.fori_loop(0, groups_out, spread_got, 0)

    for ch in range(CHUNKS):
        for copy in halos[ch]:
            copy.wait()

        for part in range(imported // GROUP):
            tiles = []
            for n in range(part * GROUP, (part + 1) * GROUP):
                tile = spec_got[ch, n // capacity, n % capacity]
                tiles.append((tile[:REP], tile[REP:]))
            prepare(ch, tiles, events + part * GROUP)

        if ch:
            rbuf_b[...] = jnp.zeros_like(rbuf_b)
        stage_a(ch, 0, cross_a, quad_a)
        pairs = events // 2

        def two_pairs(i, c, ch=ch):
            p = 2 * i
            stage_a(ch, p + 1, cross_b, quad_b)
            stage_b(ch, p, cross_a, quad_a, rbuf_a, gbuf_a)
            stage_c(ch, jnp.maximum(p - 1, 0), rbuf_b, gbuf_b)
            stage_a(ch, jnp.minimum(p + 2, pairs - 1), cross_a, quad_a)
            stage_b(ch, p + 1, cross_b, quad_b, rbuf_b, gbuf_b)
            stage_c(ch, p, rbuf_a, gbuf_a)
            return c

        lax.fori_loop(0, pairs // 2, two_pairs, 0)
        stage_c(ch, pairs - 1, rbuf_b, gbuf_b)

    share = off_ref.shape[0] // sta_n

    def off_copy(d):
        return pltpu.make_async_remote_copy(
            src_ref=off_ref.at[pl.ds(sta_at[d] * share, share)], dst_ref=off_got.at[d - 1],
            send_sem=off_ss.at[d - 1], recv_sem=off_rs.at[d - 1],
            device_id=(sta_at[d], me_c), device_id_type=MESH,
        )

    off_copies = [off_copy(d) for d in range(1, sta_n)]
    for copy in off_copies:
        copy.start()

    lane_out = lax.broadcasted_iota(jnp.int32, (cands, 128), 1)
    pad = jnp.zeros((imported, 128), F32)
    geo_t = geo_ref.reshape(rows * 8 * CHUNKS, 128)
    partial_sums = [None] * 20
    for ch in range(CHUNKS):
        totals = []
        for n in range(4):
            own = jnp.concatenate([own_ref[ch, n], pad], axis=0)
            part = acc_ref[ch, :, n * 128 : (n + 1) * 128]
            totals.append(part + own if n < 2 else own - part)
        geos = [geo_t[pl.ds(8 * ch + n, cands, stride=8 * CHUNKS), :] for n in range(8)]
        for i in range(4):
            scaled = [totals[h] * geos[4 * h + i] for h in range(2)]
            for j in range(i, 5):
                if j < 4:
                    term = scaled[0] * geos[j] + scaled[1] * geos[4 + j]
                else:
                    term = totals[2] * geos[i] + totals[3] * geos[4 + i]
                n = 5 * i + j
                partial_sums[n] = term if ch == 0 else partial_sums[n] + term
    result = jnp.zeros((cands, 128), F32)
    for i in range(4):
        for j in range(i, 5):
            value = jnp.sum(partial_sums[5 * i + j], axis=1, keepdims=True)
            keep = lane_out == 8 * i + j
            if j < 4:
                keep = keep | (lane_out == 8 * j + i)
            result = jnp.where(keep, value, result)
    result = jnp.concatenate([result, jnp.zeros((128 - cands, 128), F32)], axis=0).T
    for x in range(sta_n):
        side_ref[x] = result[8 * x : 8 * x + 8]

    def side_copy(n):
        d, h = peers[n]
        return pltpu.make_async_remote_copy(
            src_ref=side_ref.at[sta_at[d]], dst_ref=side_got.at[n],
            send_sem=side_ss.at[n], recv_sem=side_rs.at[n],
            device_id=(sta_at[d], clu_back[h]), device_id_type=MESH,
        )

    side_copies = [side_copy(n) for n in range(len(peers))]
    for copy in side_copies:
        copy.start()
    for copy in off_copies:
        copy.wait()
    total = off_ref[pl.ds(pl.multiple_of(me_s * share, share), share), :]
    for d in range(1, sta_n):
        total = total + off_got[d - 1]
    for ij in range(share // PAD_K):
        for u in range(GROUP):
            count = len(range(u, neighbours, GROUP))
            block = total[ij * PAD_K : ij * PAD_K + PAD_K, u * 32 : u * 32 + 32]
            last_ref[pl.ds(ij * 128 + 1 + u, count, stride=GROUP), 0:32] = block[:count]
    for copy in side_copies:
        copy.wait()

    kept = side_ref[me_s]
    for n, (d, h) in enumerate(peers):
        if h == groups_out:
            kept = kept + side_got[n]
    away = jnp.zeros((8, 128), F32)
    for h in range(groups_out):
        part = jnp.zeros((8, 128), F32)
        for n, (d, g) in enumerate(peers):
            if g == h:
                part = part + side_got[n]
        lowest = events + h * capacity
        away = jnp.where((lane8 >= lowest) & (lane8 < lowest + capacity), part, away)
    owner_row = jnp.full((1, 128), -1, jnp.int32)
    for h in range(groups_out):
        lowest = events + h * capacity
        inside = (lane8[0:1] >= lowest) & (lane8[0:1] < lowest + capacity)
        owner_row = jnp.where(inside, pltpu.roll(exports_row[h : h + 1, :], lowest, 1), owner_row)
    owner = jnp.where(
        lax.broadcasted_iota(jnp.int32, (events, 128), 0) == owner_row, 1.0, 0.0
    ).astype(BF16)
    back = jnp.zeros((8, events), F32)
    for _ in range(3):
        piece = away.astype(BF16)
        back = back + lax.dot_general(piece, owner, NT, preferred_element_type=F32)
        away = away - piece.astype(F32)
    side = kept[:, :events] + back
    right_out[...] = side[4:5]
    for ij in range(share // PAD_K):
        last_ref[ij * 128 : ij * 128 + 1, 0:32] = side[ij : ij + 1]
        off_out[ij] = last_ref[ij * 128 : ij * 128 + 128, :].T[:events, : neighbours + 1]


def on_device(spectra, partials, pair_list, station_mask, exports):
    events, stations, two_freq = spectra.shape
    sta_n, clu_n = lax.axis_size("sta"), lax.axis_size("clu")
    groups_out, capacity = exports.shape
    half_span = groups_out // 2
    neighbours = pair_list.shape[1]
    imported = groups_out * capacity
    cands = events + imported
    rows = cands + 1
    offsets = [h - half_span + (1 if h >= half_span else 0) for h in range(groups_out)]
    n_peers = sta_n * (groups_out + 1) - 1
    masks = station_mask.transpose(1, 0, 2).reshape(neighbours * events, stations)
    smem = pl.BlockSpec(memory_space=pltpu.SMEM)
    vmem = pl.BlockSpec(memory_space=pltpu.VMEM)
    dma = pltpu.SemaphoreType.DMA
    share = 16 * PAD_K // sta_n
    off, right = pl.pallas_call(
        functools.partial(kernel, offsets, (events, neighbours, sta_n, clu_n, stations * sta_n)),
        out_shape=(
            jax.ShapeDtypeStruct((16 // sta_n, events, neighbours + 1), F32),
            jax.ShapeDtypeStruct((1, events), F32),
        ),
        in_specs=[smem, smem] + [pl.BlockSpec(memory_space=pl.ANY)] * 6,
        out_specs=(vmem, vmem),
        scratch_shapes=[
            pltpu.VMEM(spectra.shape, BF16),
            pltpu.VMEM(partials.shape, BF16),
            pltpu.VMEM(pair_list.shape, jnp.int32),
            pltpu.VMEM(exports.shape, jnp.int32),
            pltpu.VMEM(masks.shape, jnp.int32),
            pltpu.VMEM((2 * two_freq, 5 * two_freq), BF16),
            pltpu.VMEM((8, 128), jnp.int32),
            dma((6,)),
            pltpu.VMEM((CHUNKS, groups_out, capacity, 2 * REP, two_freq), BF16),
            pltpu.VMEM((CHUNKS, groups_out, capacity, 2 * REP, two_freq), BF16),
            pltpu.VMEM((groups_out, capacity, 4, stations), BF16),
            pltpu.VMEM((groups_out, capacity, 4, stations), BF16),
            pltpu.VMEM((CHUNKS, rows, REP, 128), F32),
            pltpu.VMEM((CHUNKS, rows, REP, 128), F32),
            pltpu.VMEM((CHUNKS, rows, REP, 128), F32),
            pltpu.VMEM((CHUNKS, rows, 8, 128), F32),
            pltpu.VMEM((rows, 8 * CHUNKS, 128), F32),
            pltpu.VMEM((events, 128), F32),
            pltpu.VMEM((16 * PAD_K, 256), F32),
            pltpu.VMEM((CHUNKS, cands, 512), F32),
            pltpu.VMEM((CHUNKS, 4, events, 128), F32),
            pltpu.VMEM((sta_n, 8, 128), F32),
            pltpu.VMEM((sta_n - 1, share, 256), F32),
            pltpu.VMEM((n_peers, 8, 128), F32),
            pltpu.VMEM((16 // sta_n * 128, 128), F32),
            pltpu.VMEM((2 * neighbours * REP, 256), BF16),
            pltpu.VMEM((2 * neighbours * REP, 256), BF16),
            pltpu.VMEM((2 * neighbours * REP, 128), BF16),
            pltpu.VMEM((2 * neighbours * REP, 128), BF16),
            pltpu.VMEM((2, PAD_K * 16, 128), F32),
            pltpu.VMEM((2, PAD_K * 16, 128), F32),
            pltpu.VMEM((2, PAD_K * 16, 128), F32),
            pltpu.VMEM((2, PAD_K * 16, 128), F32),
            pltpu.VMEM((CHUNKS, events, 16, 128), F32),
            pltpu.VMEM((events // 2, cands, 128), BF16),
            pltpu.VMEM((events // 2, 256, 256), BF16),
            dma((CHUNKS, groups_out)), dma((CHUNKS, groups_out)), dma((groups_out,)), dma((groups_out,)),
            dma((sta_n - 1,)), dma((sta_n - 1,)), dma((n_peers,)), dma((n_peers,)),
        ],
        compiler_params=pltpu.CompilerParams(
            vmem_limit_bytes=60 << 20, collective_id=0, has_side_effects=True
        ),
    )(
        exports, pair_list, spectra, partials, pair_list, exports, masks,
        jnp.asarray(moment_tables(two_freq // 2)),
    )
    return (off.transpose(0, 2, 1), right)


def solution(mesh):
    return jax.shard_map(
        on_device,
        mesh=mesh,
        in_specs=(
            P("clu", "sta", None),
            P("clu", None, "sta"),
            P("clu", None),
            P("clu", None, "sta"),
            P("clu", None),
        ),
        out_specs=(P("sta", None, "clu"), P("sta", "clu")),
        check_vma=False,
    )
```

time: 76.2 us -> 69.1 us (0.907)
  Pallas kernels: 71.3 us -> 66.2 us
  local copies, waits for them, and re-layouts: 3.9 us -> 1.99 us
    pallas_call x1, Pallas kernels: 71.3 us -> 66.2 us  [on_device(): pl.pallas_call(functools.partial(kernel, offsets, (events, neighbours, st...]
    reshape x2 -> x0, local copies, waits for them, and re-layouts: 0.85 us -> none  [the longest x1 0.77 us: on_device(): exports.reshape(1, -1)]
    unnamed x18 -> x4, local copies, waits for them, and re-layouts: 2.46 us -> 1.99 us
where the time goes in v2:
time: 69.1 us; the launch traced here: 68.8 us
  Pallas kernels  66.2 us (96%)
  local copies, waits for them, and re-layouts  1.99 us (3%)
    pallas_call x1, Pallas kernels, on_device(): pl.pallas_call(functools.partial(kernel, offsets, (events, neighbours, st...  66.2 us
    unnamed x4, local copies, waits for them, and re-layouts  1.99 us

profile of v2, /device:TPU:1, one launch (start us, length us, event | category | flops | bytes accessed | tf_op | source)
XLA Modules:
  0.0 68.8 jit_solution(17621421034894009737)
XLA Ops:
  0.6 66.2 %shard_map.77 = (f32[4,32,51]{2,1,0:T(8,128)}, f32[1,32]{1,0:T(1,128)}) custom-call(s32[6,12]{1,0:T(8,128)} %exports_hbm.1, s32[32,50]{1,0:T(8,128)} %pairs_hbm.1, bf16[32,64,128]{2,1,0:T(8,128)(2,1)} %spec_hbm.1, bf16[32,4,64]{2,1,0:T(4,128)(2,1)} %geo_hbm.1, s32[32,50]{1,0:T(8,128)} %pairs_hbm.1, s32[6,12]{1,0:T(8,128)} %exports_hbm.1, ...), custom_call_target="tpu_custom_call" | custom-call | tf_op jit(solution)/shard_map/pallas_call | solution.py:471
  66.8 0.0 copy-start
  66.9 1.5 %copy.10 = f32[4,51,32]{1,2,0:T(8,128)} copy(f32[4,51,32]{1,2,0:T(8,128)} %bitcast.5) | data formatting | bytes 52224
  68.3 0.0 copy-done
  68.3 0.5 copy.11
Async XLA Ops:
  66.8 1.5 %copy-start = (f32[1,32]{1,0:T(1,128)S(1)}, f32[1,32]{1,0:T(1,128)}, u32[]{:S(2)}) copy-start(f32[1,32]{1,0:T(1,128)} %get-tuple-element.9) | copy-start | bytes 388

commit v3 on v2

--- a/solution.py
+++ b/solution.py
@@ -126,7 +126,7 @@
     order_h = sorted(range(groups_out), key=lambda h: -abs(offsets[h]))
     geo_halos = [geo_halo(h) for h in order_h]
     halos = [[halo(ch, h) for h in order_h] for ch in range(CHUNKS)]
-    for copy in geo_halos + sum(halos, []):
+    for copy in geo_halos + halos[0]:
         copy.start()
 
     block8 = lax.broadcasted_iota(jnp.int32, (8, 128), 1) // REP
@@ -325,6 +325,8 @@
     for ch in range(CHUNKS):
         for copy in halos[ch]:
             copy.wait()
+        for copy in halos[ch + 1] if ch + 1 < CHUNKS else []:
+            copy.start()
 
         for part in range(imported // GROUP):
             tiles = []

time: 69.1 us -> 66.6 us (0.964)
  Pallas kernels: 66.2 us -> 63.7 us
    pallas_call x1, Pallas kernels: 66.2 us -> 63.7 us  [on_device(): pl.pallas_call(functools.partial(kernel, offsets, (events, neighbours, st...]
where the time goes in v3:
time: 66.6 us; the launch traced here: 66.4 us
  Pallas kernels  63.7 us (96%)
  local copies, waits for them, and re-layouts  1.99 us (3%)
    pallas_call x1, Pallas kernels, on_device(): pl.pallas_call(functools.partial(kernel, offsets, (events, neighbours, st...  63.7 us
    unnamed x4, local copies, waits for them, and re-layouts  1.99 us

profile of v3, /device:TPU:1, one launch (start us, length us, event | category | flops | bytes accessed | tf_op | source)
XLA Modules:
  0.0 66.4 jit_solution(15826866647250396685)
XLA Ops:
  0.6 63.7 %shard_map.77 = (f32[4,32,51]{2,1,0:T(8,128)}, f32[1,32]{1,0:T(1,128)}) custom-call(s32[6,12]{1,0:T(8,128)} %exports_hbm.1, s32[32,50]{1,0:T(8,128)} %pairs_hbm.1, bf16[32,64,128]{2,1,0:T(8,128)(2,1)} %spec_hbm.1, bf16[32,4,64]{2,1,0:T(4,128)(2,1)} %geo_hbm.1, s32[32,50]{1,0:T(8,128)} %pairs_hbm.1, s32[6,12]{1,0:T(8,128)} %exports_hbm.1, ...), custom_call_target="tpu_custom_call" | custom-call | tf_op jit(solution)/shard_map/pallas_call | solution.py:473
  64.4 0.0 copy-start
  64.4 1.5 %copy.10 = f32[4,51,32]{1,2,0:T(8,128)} copy(f32[4,51,32]{1,2,0:T(8,128)} %bitcast.5) | data formatting | bytes 52224
  65.9 0.0 copy-done
  65.9 0.5 copy.11
Async XLA Ops:
  64.4 1.5 %copy-start = (f32[1,32]{1,0:T(1,128)S(1)}, f32[1,32]{1,0:T(1,128)}, u32[]{:S(2)}) copy-start(f32[1,32]{1,0:T(1,128)} %get-tuple-element.9) | copy-start | bytes 388
